TPU v7x, 256 devices: a whole 4x4x8 slice. The times are simulated.
256 devices in a mesh: pipe: 4 (over x), dp: 64 (over z, y, core).
Axes of the slice: x: 4, y: 4, z: 8, core: 2. Of those that a mesh axis runs over, the one named last changes fastest.
Arguments:
- hidden: bfloat16 [4, 2048, 3072], P(None, 'dp'), may hold values from -6 to 6
- w_query: bfloat16 [4, 2, 3072, 1536], P('pipe', None, 'dp'), may hold values from -0.109375 to 0.109375
- w_key: bfloat16 [4, 2, 3072, 1536], P('pipe', None, 'dp'), may hold values from -0.109375 to 0.109375
- w_value: bfloat16 [4, 2, 3072, 1536], P('pipe', None, 'dp'), may hold values from -0.109375 to 0.109375
- w_out: bfloat16 [4, 2, 1536, 3072], P('pipe', None, None, 'dp'), may hold values from -0.15625 to 0.15625
- video_len: int32 [4, 16], replicated, may hold values from 1 to 96
- audio_len: int32 [4, 16], replicated, may hold values from 1 to 32
Outputs:
- final: bfloat16 [4, 2048, 3072], P('pipe', 'dp')
All inputs are finite; a program needn't handle non-finite values.
Results may differ from a plain program's by a relative error of at most 0.017.
Values may be sent and summed in bfloat16 or wider, within the bound.
No kernel may reach another device: no remote copies, remote signals or barrier semaphores. Data moves between devices by JAX's collectives and lax.ppermute only.
A program may use at most 128 MiB of HBM per device.

v0:
```python
import jax
import jax.numpy as jnp
from jax import lax
from jax.sharding import PartitionSpec as P

HEAD = 128


def from_partner(block, axis, bit):
    count = lax.axis_size(axis)
    route = []
    for low in range(count):
        high = low | 1 << bit
        if high != low and high < count:
            route += [(low, high), (high, low)]
    return lax.ppermute(block, axis, route)


def shifted(value, axis, steps):
    count = lax.axis_size(axis)
    first, last = (max(0, -steps), min(count, count - steps))
    return lax.ppermute(value, axis, [(source, source + steps) for source in range(first, last)])


def rms_norm(values):
    wide = values.astype(jnp.float32)
    scale = lax.rsqrt(jnp.mean(wide * wide, axis=-1, keepdims=True) + 1e-06)
    return (wide * scale).astype(jnp.bfloat16)


def project(rows, weight, factor):
    return (jnp.dot(rows, weight, preferred_element_type=jnp.float32) * factor).astype(jnp.bfloat16)


def project_back(rows, weight_t):
    return lax.dot_general(
        rows, weight_t, (((1,), (1,)), ((), ())), preferred_element_type=jnp.float32
    )


def attend(query, keys, values, valid):
    queries = query.shape[0]
    kcount = keys.shape[0]
    width = query.shape[1]
    heads = width // HEAD
    shaped_query = query.reshape(queries, heads, HEAD)
    shaped_keys = keys.reshape(kcount, heads, HEAD)
    shaped_values = values.reshape(kcount, heads, HEAD)
    scores = jnp.einsum(
        "qhd,khd->hqk", shaped_query, shaped_keys, preferred_element_type=jnp.float32
    )
    scores = jnp.where(valid[None, None, :], scores, -1e30)
    weights = jax.nn.softmax(scores, axis=-1).astype(jnp.bfloat16)
    attended = jnp.einsum(
        "hqk,khd->qhd", weights, shaped_values, preferred_element_type=jnp.float32
    )
    return attended.astype(jnp.bfloat16).reshape(queries, width)


def share_group(normed, place):
    low_bit = place % 2
    high_bit = place // 2
    partner = from_partner(normed, "dp", 0)
    paired = jnp.where(
        low_bit == 0, jnp.concatenate([normed, partner]), jnp.concatenate([partner, normed])
    )
    distant = from_partner(paired, "dp", 1)
    return jnp.where(
        high_bit == 0, jnp.concatenate([paired, distant]), jnp.concatenate([distant, paired])
    )


def reduce_group(partial_value, place):
    row_count = partial_value.shape[0] // 4
    high_bit = place // 2
    low_bit = place % 2
    halves = partial_value.reshape(2, 2 * row_count, partial_value.shape[1])
    mine = jnp.where(high_bit == 0, halves[0], halves[1])
    other = jnp.where(high_bit == 0, halves[1], halves[0])
    arrived = from_partner(other, "dp", 1)
    pair_sum = mine.astype(jnp.float32) + arrived.astype(jnp.float32)
    quarters = pair_sum.reshape(2, row_count, partial_value.shape[1])
    kept = jnp.where(low_bit == 0, quarters[0], quarters[1])
    given = jnp.where(low_bit == 0, quarters[1], quarters[0])
    back = from_partner(given.astype(jnp.bfloat16), "dp", 0).astype(given.dtype)
    return kept + back


def spread_columns(weight, count):
    towers, rows, cols = weight.shape
    quarter = cols // 4
    parts = jnp.transpose(weight.reshape(towers, rows, 4, quarter), (0, 2, 1, 3))
    parts = jnp.broadcast_to(parts[:, None], (towers, count // 4, 4, rows, quarter))
    return parts.reshape(towers, count, rows, quarter)


def body(hidden, w_query, w_key, w_value, w_out, video_len, audio_len):
    count = lax.axis_size("dp")
    sections = lax.axis_size("pipe")
    rank = lax.axis_index("dp")
    section = lax.axis_index("pipe")
    place = rank % 4
    group = rank // 4
    batches, row_count, width = hidden.shape
    features = w_query.shape[3]
    quarter = features // 4
    factor = HEAD ** (-0.5)
    got_query, got_key, got_value = (
        lax.all_to_all(
            spread_columns(w_query[0], count), "dp", split_axis=1, concat_axis=1, tiled=True
        ),
        lax.all_to_all(
            spread_columns(w_key[0], count), "dp", split_axis=1, concat_axis=1, tiled=True
        ),
        lax.all_to_all(
            spread_columns(w_value[0], count), "dp", split_axis=1, concat_axis=1, tiled=True
        ),
    )
    got_query = got_query.reshape(2, width, quarter)
    got_key = got_key.reshape(2, width, quarter)
    got_value = got_value.reshape(2, width, quarter)
    out_cols = w_out.shape[3]
    parts = jnp.transpose(w_out[0].reshape(2, 4, quarter, out_cols), (0, 1, 3, 2))
    parts = jnp.broadcast_to(parts[:, None], (2, count // 4, 4, out_cols, quarter)).reshape(
        2, count, out_cols, quarter
    )
    got_out = lax.all_to_all(parts, "dp", split_axis=1, concat_axis=1, tiled=True)
    quarter_out = got_out.reshape(2, width, quarter)
    audio_index = jnp.arange(row_count, dtype=jnp.int32)
    video_index = jnp.arange(3 * row_count, dtype=jnp.int32)
    results = jnp.zeros((batches, row_count, width), jnp.bfloat16)
    incoming = jnp.zeros((row_count, width), jnp.bfloat16)
    total_steps = batches + sections - 1
    for step in range(total_steps):
        offset = step - section
        batch = jnp.clip(offset, 0, batches - 1)
        fresh = hidden[min(step, batches - 1)]
        current = jnp.where(section == 0, fresh, incoming)
        video_count = video_len[batch, group]
        audio_count = audio_len[batch, group]
        normed = rms_norm(current)
        quad = share_group(normed, place)
        video_rows = quad[: 3 * row_count]
        audio_rows = quad[3 * row_count :]
        video_query = project(video_rows, got_query[0], factor)
        audio_query = project(audio_rows, got_query[1], factor)
        video_key = project(audio_rows, got_key[0], 1.0)
        video_value = project(audio_rows, got_value[0], 1.0)
        audio_key = project(video_rows, got_key[1], 1.0)
        audio_value = project(video_rows, got_value[1], 1.0)
        video_att = attend(video_query, video_key, video_value, audio_index < audio_count)
        audio_att = attend(audio_query, audio_key, audio_value, video_index < video_count)
        video_part = project_back(video_att, quarter_out[0])
        audio_part = project_back(audio_att, quarter_out[1])
        partial_value = jnp.concatenate([video_part, audio_part]).astype(jnp.bfloat16)
        update = reduce_group(partial_value, place)
        done = (current.astype(jnp.float32) + update).astype(jnp.bfloat16)
        keep = (section == sections - 1) & (offset >= 0) & (offset < batches)
        results = jnp.where(keep, lax.dynamic_update_index_in_dim(results, done, batch, 0), results)
        if step + 1 < total_steps:
            incoming = shifted(done, "pipe", 1)
    delivered = lax.all_to_all(results, "pipe", split_axis=0, concat_axis=0, tiled=True)
    share = batches // sections
    return delivered[(sections - 1) * share :]


def solution(mesh):
    return jax.shard_map(
        body,
        mesh=mesh,
        in_specs=(
            P(None, "dp", None),
            P("pipe", None, "dp", None),
            P("pipe", None, "dp", None),
            P("pipe", None, "dp", None),
            P("pipe", None, None, "dp"),
            P(),
            P(),
        ),
        out_specs=P("pipe", "dp", None),
        check_vma=False,
    )
```

profile of v0, /device:TPU:56, one launch (start us, length us, event | category | flops | bytes accessed | tf_op | source)
XLA Modules:
  0.0 828.3 jit_solution(6810401134842873065)
XLA Ops:
  3.9 11.7 %all-to-all-start.2 = ((bf16[2,64,48,384]{3,2,0,1:T(8,128)(2,1)}), bf16[2,64,48,384]{3,2,0,1:T(8,128)(2,1)}, u32[]{:S(2)}, u32[]{:S(2)}) async-start(bf16[2,64,48,384]{3,2,0,1:T(8,128)(2,1)} %bitcast.538), calls=%async_computation.2 | async-start | bytes 9437184 | tf_op jit(solution)/shard_map/all_to_all | solution.py:112
  15.7 106.4 %all-to-all-done.2 = bf16[2,64,48,384]{3,2,0,1:T(8,128)(2,1)} async-done(((bf16[2,64,48,384]{3,2,0,1:T(8,128)(2,1)}), bf16[2,64,48,384]{3,2,0,1:T(8,128)(2,1)}, u32[]{:S(2)}, u32[]{:S(2)}) %all-to-all-start.2) | async-done | bytes 4718624 | tf_op jit(solution)/shard_map/all_to_all | solution.py:112
  124.9 6.8 all-to-all-start.1
  131.8 106.4 %all-to-all-done.1 = bf16[2,64,48,384]{3,2,0,1:T(8,128)(2,1)} async-done(((bf16[2,64,48,384]{3,2,0,1:T(8,128)(2,1)}), bf16[2,64,48,384]{3,2,0,1:T(8,128)(2,1)}, u32[]{:S(2)}, u32[]{:S(2)}) %all-to-all-start.1) | async-done | bytes 4718624 | tf_op jit(solution)/shard_map/all_to_all | solution.py:109
  241.0 6.8 all-to-all-start
  247.9 106.4 %all-to-all-done = bf16[2,64,48,384]{3,2,0,1:T(8,128)(2,1)} async-done(((bf16[2,64,48,384]{3,2,0,1:T(8,128)(2,1)}), bf16[2,64,48,384]{3,2,0,1:T(8,128)(2,1)}, u32[]{:S(2)}, u32[]{:S(2)}) %all-to-all-start) | async-done | bytes 4718624 | tf_op jit(solution)/shard_map/all_to_all | solution.py:115
  357.1 6.8 all-to-all-start.3
  368.9 21.6 %collective-permute-done.1 = bf16[64,3072]{1,0:T(8,128)(2,1)S(1)} collective-permute-done((bf16[64,3072]{1,0:T(8,128)(2,1)S(1)}, bf16[64,3072]{1,0:T(8,128)(2,1)S(1)}, u32[]{:S(2)}, u32[]{:S(2)}) %collective-permute-start.1) | collective-permute-done | bytes 393248 | tf_op jit(solution)/shard_map/ppermute | solution.py:16
  394.0 4.6 fusion.316
  409.4 61.1 %all-to-all-done.3 = bf16[2,64,48,384]{3,2,0,1:T(8,128)(2,1)} async-done(((bf16[2,64,48,384]{3,2,0,1:T(8,128)(2,1)}), bf16[2,64,48,384]{3,2,0,1:T(8,128)(2,1)}, u32[]{:S(2)}, u32[]{:S(2)}) %all-to-all-start.3) | async-done | bytes 4718624 | tf_op jit(solution)/shard_map/all_to_all | solution.py:127
  481.0 10.1 %collective-permute-done.2 = bf16[64,3072]{1,0:T(8,128)(2,1)S(1)} collective-permute-done((bf16[64,3072]{1,0:T(8,128)(2,1)S(1)}, bf16[64,3072]{1,0:T(8,128)(2,1)S(1)}, u32[]{:S(2)}, u32[]{:S(2)}) %collective-permute-start.2) | collective-permute-done | bytes 393248 | tf_op jit(solution)/shard_map/ppermute | solution.py:16
  498.7 4.4 collective-permute-done.4
  508.3 9.1 %collective-permute-done.6 = bf16[64,3072]{1,0:T(8,128)(2,1)S(1)} collective-permute-done((bf16[64,3072]{1,0:T(8,128)(2,1)S(1)}, bf16[64,3072]{1,0:T(8,128)(2,1)S(1)}, u32[]{:S(2)}, u32[]{:S(2)}) %collective-permute-start.6) | collective-permute-done | bytes 393248 | tf_op jit(solution)/shard_map/ppermute | solution.py:16
  533.3 9.6 %collective-permute-done.7 = bf16[64,3072]{1,0:T(8,128)(2,1)S(1)} collective-permute-done((bf16[64,3072]{1,0:T(8,128)(2,1)S(1)}, bf16[64,3072]{1,0:T(8,128)(2,1)S(1)}, u32[]{:S(2)}, u32[]{:S(2)}) %collective-permute-start.7) | collective-permute-done | bytes 393248 | tf_op jit(solution)/shard_map/ppermute | solution.py:16
  552.1 4.4 collective-permute-done.9
  561.3 9.3 %collective-permute-done.11 = bf16[64,3072]{1,0:T(8,128)(2,1)S(1)} collective-permute-done((bf16[64,3072]{1,0:T(8,128)(2,1)S(1)}, bf16[64,3072]{1,0:T(8,128)(2,1)S(1)}, u32[]{:S(2)}, u32[]{:S(2)}) %collective-permute-start.11) | collective-permute-done | bytes 393248 | tf_op jit(solution)/shard_map/ppermute | solution.py:16
  586.4 9.6 %collective-permute-done.12 = bf16[64,3072]{1,0:T(8,128)(2,1)S(1)} collective-permute-done((bf16[64,3072]{1,0:T(8,128)(2,1)S(1)}, bf16[64,3072]{1,0:T(8,128)(2,1)S(1)}, u32[]{:S(2)}, u32[]{:S(2)}) %collective-permute-start.12) | collective-permute-done | bytes 393248 | tf_op jit(solution)/shard_map/ppermute | solution.py:16
  601.2 4.4 collective-permute-start.14
  605.6 4.4 collective-permute-done.14
  615.0 9.2 %collective-permute-done.16 = bf16[64,3072]{1,0:T(8,128)(2,1)S(1)} collective-permute-done((bf16[64,3072]{1,0:T(8,128)(2,1)S(1)}, bf16[64,3072]{1,0:T(8,128)(2,1)S(1)}, u32[]{:S(2)}, u32[]{:S(2)}) %collective-permute-start.16) | collective-permute-done | bytes 393248 | tf_op jit(solution)/shard_map/ppermute | solution.py:16
  640.0 9.6 %collective-permute-done.17 = bf16[64,3072]{1,0:T(8,128)(2,1)S(1)} collective-permute-done((bf16[64,3072]{1,0:T(8,128)(2,1)S(1)}, bf16[64,3072]{1,0:T(8,128)(2,1)S(1)}, u32[]{:S(2)}, u32[]{:S(2)}) %collective-permute-start.17) | collective-permute-done | bytes 393248 | tf_op jit(solution)/shard_map/ppermute | solution.py:16
  654.4 4.4 collective-permute-start.19
  658.8 4.4 collective-permute-done.19
  668.2 9.3 %collective-permute-done.21 = bf16[64,3072]{1,0:T(8,128)(2,1)S(1)} collective-permute-done((bf16[64,3072]{1,0:T(8,128)(2,1)S(1)}, bf16[64,3072]{1,0:T(8,128)(2,1)S(1)}, u32[]{:S(2)}, u32[]{:S(2)}) %collective-permute-start.21) | collective-permute-done | bytes 393248 | tf_op jit(solution)/shard_map/ppermute | solution.py:16
  693.4 9.6 %collective-permute-done.22 = bf16[64,3072]{1,0:T(8,128)(2,1)S(1)} collective-permute-done((bf16[64,3072]{1,0:T(8,128)(2,1)S(1)}, bf16[64,3072]{1,0:T(8,128)(2,1)S(1)}, u32[]{:S(2)}, u32[]{:S(2)}) %collective-permute-start.22) | collective-permute-done | bytes 393248 | tf_op jit(solution)/shard_map/ppermute | solution.py:16
  712.2 4.4 collective-permute-done.24
  721.5 9.2 %collective-permute-done.26 = bf16[64,3072]{1,0:T(8,128)(2,1)S(1)} collective-permute-done((bf16[64,3072]{1,0:T(8,128)(2,1)S(1)}, bf16[64,3072]{1,0:T(8,128)(2,1)S(1)}, u32[]{:S(2)}, u32[]{:S(2)}) %collective-permute-start.26) | collective-permute-done | bytes 393248 | tf_op jit(solution)/shard_map/ppermute | solution.py:16
  746.5 9.6 %collective-permute-done.27 = bf16[64,3072]{1,0:T(8,128)(2,1)S(1)} collective-permute-done((bf16[64,3072]{1,0:T(8,128)(2,1)S(1)}, bf16[64,3072]{1,0:T(8,128)(2,1)S(1)}, u32[]{:S(2)}, u32[]{:S(2)}) %collective-permute-start.27) | collective-permute-done | bytes 393248 | tf_op jit(solution)/shard_map/ppermute | solution.py:16
  765.5 4.4 collective-permute-done.29
  774.8 9.3 %collective-permute-done.31 = bf16[64,3072]{1,0:T(8,128)(2,1)S(1)} collective-permute-done((bf16[64,3072]{1,0:T(8,128)(2,1)S(1)}, bf16[64,3072]{1,0:T(8,128)(2,1)S(1)}, u32[]{:S(2)}, u32[]{:S(2)}) %collective-permute-start.31) | collective-permute-done | bytes 393248 | tf_op jit(solution)/shard_map/ppermute | solution.py:16
  798.2 9.6 %collective-permute-done.32 = bf16[64,3072]{1,0:T(8,128)(2,1)S(1)} collective-permute-done((bf16[64,3072]{1,0:T(8,128)(2,1)S(1)}, bf16[64,3072]{1,0:T(8,128)(2,1)S(1)}, u32[]{:S(2)}, u32[]{:S(2)}) %collective-permute-start.32) | collective-permute-done | bytes 393248 | tf_op jit(solution)/shard_map/ppermute | solution.py:16
  809.7 17.7 %all_to_all.25 = bf16[4,32,3072]{2,1,0:T(8,128)(2,1)S(1)} all-to-all(bf16[4,32,3072]{2,1,0:T(8,128)(2,1)S(1)} %fusion.156), channel_id=1, replica_groups=mesh['pipe'=4,'dp'=64] {'pipe'}, dimensions={0} | all-to-all | bytes 1572864 | tf_op jit(solution)/shard_map/all_to_all | solution.py:162
  (328 shorter events, 211.8 us)
Async XLA Ops:
  3.9 118.3 %all-to-all-start.2 = ((bf16[2,64,48,384]{3,2,0,1:T(8,128)(2,1)}), bf16[2,64,48,384]{3,2,0,1:T(8,128)(2,1)}, u32[]{:S(2)}, u32[]{:S(2)}) async-start(bf16[2,64,48,384]{3,2,0,1:T(8,128)(2,1)} %bitcast.538), calls=%async_computation.2 | async-start | bytes 9437184 | tf_op jit(solution)/shard_map/all_to_all | solution.py:112
  124.9 113.4 %all-to-all-start.1 = ((bf16[2,64,48,384]{3,2,0,1:T(8,128)(2,1)}), bf16[2,64,48,384]{3,2,0,1:T(8,128)(2,1)}, u32[]{:S(2)}, u32[]{:S(2)}) async-start(bf16[2,64,48,384]{3,2,0,1:T(8,128)(2,1)} %bitcast.539), calls=%async_computation.1 | async-start | bytes 9437184 | tf_op jit(solution)/shard_map/all_to_all | solution.py:109
  241.0 113.3 %all-to-all-start = ((bf16[2,64,48,384]{3,2,0,1:T(8,128)(2,1)}), bf16[2,64,48,384]{3,2,0,1:T(8,128)(2,1)}, u32[]{:S(2)}, u32[]{:S(2)}) async-start(bf16[2,64,48,384]{3,2,0,1:T(8,128)(2,1)} %bitcast.540), calls=%async_computation | async-start | bytes 9437184 | tf_op jit(solution)/shard_map/all_to_all | solution.py:115
  357.1 113.3 %all-to-all-start.3 = ((bf16[2,64,48,384]{3,2,0,1:T(8,128)(2,1)}), bf16[2,64,48,384]{3,2,0,1:T(8,128)(2,1)}, u32[]{:S(2)}, u32[]{:S(2)}) async-start(bf16[2,64,48,384]{3,2,0,1:T(8,128)(2,1)} %bitcast.537), calls=%async_computation.3 | async-start | bytes 9437184 | tf_op jit(solution)/shard_map/all_to_all | solution.py:127
  364.2 1.5 collective-permute-start
  365.8 24.7 %collective-permute-start.1 = (bf16[64,3072]{1,0:T(8,128)(2,1)S(1)}, bf16[64,3072]{1,0:T(8,128)(2,1)S(1)}, u32[]{:S(2)}, u32[]{:S(2)}) collective-permute-start(bf16[64,3072]{1,0:T(8,128)(2,1)S(1)} %maximum_select_fusion.7), channel_id=1, source_target_pairs={{0,2},{2,0},{1,3},{3,1},{4,6},{6,4},{5,7},{7,5},{8,10},{10,8},{9,1... | collective-permute-start | bytes 1179656 | tf_op jit(solution)/shard_map/ppermute | solution.py:16
  480.1 11.1 %collective-permute-start.2 = (bf16[64,3072]{1,0:T(8,128)(2,1)S(1)}, bf16[64,3072]{1,0:T(8,128)(2,1)S(1)}, u32[]{:S(2)}, u32[]{:S(2)}) collective-permute-start(bf16[64,3072]{1,0:T(8,128)(2,1)S(1)} %broadcast_select_fusion.6), channel_id=1, source_target_pairs={{0,2},{2,0},{1,3},{3,1},{4,6},{6,4},{5,7},{7,5},{8,10},{10,8},{9,1... | collective-permute-start | bytes 1179656 | tf_op jit(solution)/shard_map/ppermute | solution.py:16
  492.2 1.5 collective-permute-start.3
  495.3 7.9 collective-permute-start.4
  506.0 11.5 %collective-permute-start.6 = (bf16[64,3072]{1,0:T(8,128)(2,1)S(1)}, bf16[64,3072]{1,0:T(8,128)(2,1)S(1)}, u32[]{:S(2)}, u32[]{:S(2)}) collective-permute-start(bf16[64,3072]{1,0:T(8,128)(2,1)S(1)} %maximum_select_fusion.8), channel_id=1, source_target_pairs={{0,2},{2,0},{1,3},{3,1},{4,6},{6,4},{5,7},{7,5},{8,10},{10,8},{9,1... | collective-permute-start | bytes 1179656 | tf_op jit(solution)/shard_map/ppermute | solution.py:16
  532.5 10.4 %collective-permute-start.7 = (bf16[64,3072]{1,0:T(8,128)(2,1)S(1)}, bf16[64,3072]{1,0:T(8,128)(2,1)S(1)}, u32[]{:S(2)}, u32[]{:S(2)}) collective-permute-start(bf16[64,3072]{1,0:T(8,128)(2,1)S(1)} %broadcast_select_fusion.5), channel_id=1, source_target_pairs={{0,2},{2,0},{1,3},{3,1},{4,6},{6,4},{5,7},{7,5},{8,10},{10,8},{9,1... | collective-permute-start | bytes 1179656 | tf_op jit(solution)/shard_map/ppermute | solution.py:16
  544.6 1.7 collective-permute-start.8
  547.7 8.8 %collective-permute-start.9 = (bf16[32,3072]{1,0:T(8,128)(2,1)S(1)}, bf16[32,3072]{1,0:T(8,128)(2,1)S(1)}, u32[]{:S(2)}, u32[]{:S(2)}) collective-permute-start(bf16[32,3072]{1,0:T(8,128)(2,1)S(1)} %get-tuple-element.24), channel_id=1, source_target_pairs={{0,64},{64,128},{128,192},{1,65},{65,129},{129,193},{2,66},{66,130... | collective-permute-start | bytes 589832 | tf_op jit(solution)/shard_map/ppermute | solution.py:22
  559.4 11.2 %collective-permute-start.11 = (bf16[64,3072]{1,0:T(8,128)(2,1)S(1)}, bf16[64,3072]{1,0:T(8,128)(2,1)S(1)}, u32[]{:S(2)}, u32[]{:S(2)}) collective-permute-start(bf16[64,3072]{1,0:T(8,128)(2,1)S(1)} %maximum_select_fusion.9), channel_id=1, source_target_pairs={{0,2},{2,0},{1,3},{3,1},{4,6},{6,4},{5,7},{7,5},{8,10},{10,8},{9,1... | collective-permute-start | bytes 1179656 | tf_op jit(solution)/shard_map/ppermute | solution.py:16
  585.7 10.4 %collective-permute-start.12 = (bf16[64,3072]{1,0:T(8,128)(2,1)S(1)}, bf16[64,3072]{1,0:T(8,128)(2,1)S(1)}, u32[]{:S(2)}, u32[]{:S(2)}) collective-permute-start(bf16[64,3072]{1,0:T(8,128)(2,1)S(1)} %broadcast_select_fusion.4), channel_id=1, source_target_pairs={{0,2},{2,0},{1,3},{3,1},{4,6},{6,4},{5,7},{7,5},{8,10},{10,8},{9,1... | collective-permute-start | bytes 1179656 | tf_op jit(solution)/shard_map/ppermute | solution.py:16
  597.8 2.0 collective-permute-start.13
  601.2 8.8 %collective-permute-start.14 = (bf16[32,3072]{1,0:T(8,128)(2,1)S(1)}, bf16[32,3072]{1,0:T(8,128)(2,1)S(1)}, u32[]{:S(2)}, u32[]{:S(2)}) collective-permute-start(bf16[32,3072]{1,0:T(8,128)(2,1)S(1)} %get-tuple-element.20), channel_id=1, source_target_pairs={{0,64},{64,128},{128,192},{1,65},{65,129},{129,193},{2,66},{66,130... | collective-permute-start | bytes 589832 | tf_op jit(solution)/shard_map/ppermute | solution.py:22
  612.9 11.2 %collective-permute-start.16 = (bf16[64,3072]{1,0:T(8,128)(2,1)S(1)}, bf16[64,3072]{1,0:T(8,128)(2,1)S(1)}, u32[]{:S(2)}, u32[]{:S(2)}) collective-permute-start(bf16[64,3072]{1,0:T(8,128)(2,1)S(1)} %maximum_select_fusion.10), channel_id=1, source_target_pairs={{0,2},{2,0},{1,3},{3,1},{4,6},{6,4},{5,7},{7,5},{8,10},{10,8},{9,1... | collective-permute-start | bytes 1179656 | tf_op jit(solution)/shard_map/ppermute | solution.py:16
  639.3 10.4 %collective-permute-start.17 = (bf16[64,3072]{1,0:T(8,128)(2,1)S(1)}, bf16[64,3072]{1,0:T(8,128)(2,1)S(1)}, u32[]{:S(2)}, u32[]{:S(2)}) collective-permute-start(bf16[64,3072]{1,0:T(8,128)(2,1)S(1)} %broadcast_select_fusion.3), channel_id=1, source_target_pairs={{0,2},{2,0},{1,3},{3,1},{4,6},{6,4},{5,7},{7,5},{8,10},{10,8},{9,1... | collective-permute-start | bytes 1179656 | tf_op jit(solution)/shard_map/ppermute | solution.py:16
  651.4 1.7 collective-permute-start.18
  654.4 8.8 %collective-permute-start.19 = (bf16[32,3072]{1,0:T(8,128)(2,1)S(1)}, bf16[32,3072]{1,0:T(8,128)(2,1)S(1)}, u32[]{:S(2)}, u32[]{:S(2)}) collective-permute-start(bf16[32,3072]{1,0:T(8,128)(2,1)S(1)} %get-tuple-element.16), channel_id=1, source_target_pairs={{0,64},{64,128},{128,192},{1,65},{65,129},{129,193},{2,66},{66,130... | collective-permute-start | bytes 589832 | tf_op jit(solution)/shard_map/ppermute | solution.py:22
  666.1 11.4 %collective-permute-start.21 = (bf16[64,3072]{1,0:T(8,128)(2,1)S(1)}, bf16[64,3072]{1,0:T(8,128)(2,1)S(1)}, u32[]{:S(2)}, u32[]{:S(2)}) collective-permute-start(bf16[64,3072]{1,0:T(8,128)(2,1)S(1)} %maximum_select_fusion.11), channel_id=1, source_target_pairs={{0,2},{2,0},{1,3},{3,1},{4,6},{6,4},{5,7},{7,5},{8,10},{10,8},{9,1... | collective-permute-start | bytes 1179656 | tf_op jit(solution)/shard_map/ppermute | solution.py:16
  692.6 10.4 %collective-permute-start.22 = (bf16[64,3072]{1,0:T(8,128)(2,1)S(1)}, bf16[64,3072]{1,0:T(8,128)(2,1)S(1)}, u32[]{:S(2)}, u32[]{:S(2)}) collective-permute-start(bf16[64,3072]{1,0:T(8,128)(2,1)S(1)} %broadcast_select_fusion.2), channel_id=1, source_target_pairs={{0,2},{2,0},{1,3},{3,1},{4,6},{6,4},{5,7},{7,5},{8,10},{10,8},{9,1... | collective-permute-start | bytes 1179656 | tf_op jit(solution)/shard_map/ppermute | solution.py:16
  704.7 1.7 collective-permute-start.23
  707.8 8.8 %collective-permute-start.24 = (bf16[32,3072]{1,0:T(8,128)(2,1)S(1)}, bf16[32,3072]{1,0:T(8,128)(2,1)S(1)}, u32[]{:S(2)}, u32[]{:S(2)}) collective-permute-start(bf16[32,3072]{1,0:T(8,128)(2,1)S(1)} %get-tuple-element.12), channel_id=1, source_target_pairs={{0,64},{64,128},{128,192},{1,65},{65,129},{129,193},{2,66},{66,130... | collective-permute-start | bytes 589832 | tf_op jit(solution)/shard_map/ppermute | solution.py:22
  719.5 11.2 %collective-permute-start.26 = (bf16[64,3072]{1,0:T(8,128)(2,1)S(1)}, bf16[64,3072]{1,0:T(8,128)(2,1)S(1)}, u32[]{:S(2)}, u32[]{:S(2)}) collective-permute-start(bf16[64,3072]{1,0:T(8,128)(2,1)S(1)} %maximum_select_fusion.12), channel_id=1, source_target_pairs={{0,2},{2,0},{1,3},{3,1},{4,6},{6,4},{5,7},{7,5},{8,10},{10,8},{9,1... | collective-permute-start | bytes 1179656 | tf_op jit(solution)/shard_map/ppermute | solution.py:16
  745.8 10.4 %collective-permute-start.27 = (bf16[64,3072]{1,0:T(8,128)(2,1)S(1)}, bf16[64,3072]{1,0:T(8,128)(2,1)S(1)}, u32[]{:S(2)}, u32[]{:S(2)}) collective-permute-start(bf16[64,3072]{1,0:T(8,128)(2,1)S(1)} %broadcast_select_fusion.1), channel_id=1, source_target_pairs={{0,2},{2,0},{1,3},{3,1},{4,6},{6,4},{5,7},{7,5},{8,10},{10,8},{9,1... | collective-permute-start | bytes 1179656 | tf_op jit(solution)/shard_map/ppermute | solution.py:16
  757.9 1.8 collective-permute-start.28
  761.1 8.8 %collective-permute-start.29 = (bf16[32,3072]{1,0:T(8,128)(2,1)S(1)}, bf16[32,3072]{1,0:T(8,128)(2,1)S(1)}, u32[]{:S(2)}, u32[]{:S(2)}) collective-permute-start(bf16[32,3072]{1,0:T(8,128)(2,1)S(1)} %get-tuple-element.8), channel_id=1, source_target_pairs={{0,64},{64,128},{128,192},{1,65},{65,129},{129,193},{2,66},{66,130... | collective-permute-start | bytes 589832 | tf_op jit(solution)/shard_map/ppermute | solution.py:22
  772.8 11.2 %collective-permute-start.31 = (bf16[64,3072]{1,0:T(8,128)(2,1)S(1)}, bf16[64,3072]{1,0:T(8,128)(2,1)S(1)}, u32[]{:S(2)}, u32[]{:S(2)}) collective-permute-start(bf16[64,3072]{1,0:T(8,128)(2,1)S(1)} %maximum_select_fusion.13), channel_id=1, source_target_pairs={{0,2},{2,0},{1,3},{3,1},{4,6},{6,4},{5,7},{7,5},{8,10},{10,8},{9,1... | collective-permute-start | bytes 1179656 | tf_op jit(solution)/shard_map/ppermute | solution.py:16
  797.5 10.4 %collective-permute-start.32 = (bf16[64,3072]{1,0:T(8,128)(2,1)S(1)}, bf16[64,3072]{1,0:T(8,128)(2,1)S(1)}, u32[]{:S(2)}, u32[]{:S(2)}) collective-permute-start(bf16[64,3072]{1,0:T(8,128)(2,1)S(1)} %broadcast_select_fusion), channel_id=1, source_target_pairs={{0,2},{2,0},{1,3},{3,1},{4,6},{6,4},{5,7},{7,5},{8,10},{10,8},{9,1... | collective-permute-start | bytes 1179656 | tf_op jit(solution)/shard_map/ppermute | solution.py:16
  808.1 1.5 collective-permute-start.33
  (54 other events, 349.3 us)
where the time goes:
time: 836 us; the launch traced here: 828 us
  waiting for transfers between devices  573 us (69%)
  matrix products  88.9 us (11%)
  starting transfers between devices  70.5 us (8%)
  local copies, waits for them, and re-layouts  43.8 us (5%)
  other arithmetic  33.1 us (4%)
  blocking collectives  17.7 us (2%)
    ppermute x28, waiting for transfers between devices, from_partner(): return lax.ppermute(block, axis, route)  166 us
    all_to_all x1, waiting for transfers between devices, body(): lax.all_to_all(spread_columns(w_query[0], count), 'dp', split_axis=1, con...  106 us
    all_to_all x1, waiting for transfers between devices, body(): lax.all_to_all(spread_columns(w_value[0], count), 'dp', split_axis=1, con...  106 us
    all_to_all x1, waiting for transfers between devices, body(): lax.all_to_all(spread_columns(w_key[0], count), 'dp', split_axis=1, conca...  106 us
    all_to_all x1, waiting for transfers between devices, body(): lax.all_to_all(parts, 'dp', split_axis=1, concat_axis=1, tiled=True)  61.1 us
    dot_general x42, matrix products, project(): jnp.dot(rows, weight, preferred_element_type=jnp.float32) * factor  33.9 us
    dot_general x14, matrix products, project_back(): lax.dot_general(rows, weight_t, (((1,), (1,)), ((), ())), preferred_eleme...  31.8 us
    ppermute x6, waiting for transfers between devices, shifted(): lax.ppermute(value, axis, [(source, source + steps) for source in range(f...  26.6 us
  transfers between devices with their start and end apart: 38, of which 38 were waited for; matrix products, arithmetic and copies ran while one was open for 3% of the time, Pallas kernels for 0%

commit v1 on v0

v1 whole, which is shorter than its diff:
```python
import functools

import jax
import jax.numpy as jnp
from jax import lax
from jax.experimental import pallas as pl
from jax.experimental.pallas import tpu as pltpu
from jax.sharding import Mesh
from jax.sharding import PartitionSpec as P

HEAD = 128
NEAR = [(0, 1), (1, 0), (2, 3), (3, 2)]
FAR = [(1, 2), (2, 1), (3, 0), (0, 3)]
SWAP = [(0, 1), (1, 0)]


def rms_norm(values):
    wide = values.astype(jnp.float32)
    scale = lax.rsqrt(jnp.mean(wide * wide, axis=-1, keepdims=True) + 1e-06)
    return (wide * scale).astype(jnp.bfloat16)


def near(value):
    return lax.ppermute(value, "y", NEAR)


def far(value):
    return lax.ppermute(value, "y", FAR)


def swap(value):
    return lax.ppermute(value, "core", SWAP)


def attend_kernel(ctl, query, keys, values, out, *, tokens):
    rows = 4 * tokens
    flip, core = ctl[0], ctl[1]
    heads = query.shape[1] // HEAD
    key_place = lax.broadcasted_iota(jnp.int32, (rows, rows), 1) ^ flip
    query_place = lax.broadcasted_iota(jnp.int32, (rows, HEAD), 0) ^ flip
    video = 3 * tokens
    first = jnp.where(core == 0, video, 0)
    own_low = jnp.where(core == 0, 0, video)
    own_high = jnp.where(core == 0, video, rows)
    own = (query_place >= own_low) & (query_place < own_high)
    for sample in range(2):
        valid = (key_place >= first) & (key_place < first + ctl[2 + sample])
        span = pl.ds(sample * rows, rows)
        for head in range(heads):
            cols = pl.ds(head * HEAD, HEAD)
            scores = lax.dot_general(
                query[span, cols],
                keys[span, cols],
                (((1,), (1,)), ((), ())),
                preferred_element_type=jnp.float32,
            )
            scores = jnp.where(valid, scores, -1e30)
            top = jnp.max(scores, axis=-1, keepdims=True)
            powers = jnp.exp(scores - top)
            weights = (powers / jnp.sum(powers, axis=-1, keepdims=True)).astype(jnp.bfloat16)
            mixed = jnp.dot(weights, values[span, cols], preferred_element_type=jnp.float32)
            out[span, cols] = jnp.where(own, mixed, 0.0).astype(jnp.bfloat16)


def attend(ctl, query, keys, values, tokens):
    vmem = pl.BlockSpec(memory_space=pltpu.VMEM)
    return pl.pallas_call(
        functools.partial(attend_kernel, tokens=tokens),
        out_shape=jax.ShapeDtypeStruct(query.shape, jnp.bfloat16),
        in_specs=[pl.BlockSpec(memory_space=pltpu.SMEM), vmem, vmem, vmem],
        out_specs=vmem,
        cost_estimate=pl.CostEstimate(
            flops=4 * 128 * query.size, bytes_accessed=8 * query.size, transcendentals=query.size
        ),
    )(ctl, query, keys, values)


def gather_tokens(mine):
    half = mine.shape[0] // 2
    by_near, by_far = near(mine), far(mine)
    cross = jnp.concatenate([near(by_far[:half]), far(by_near[half:])])
    owned = jnp.stack([mine, by_near, cross, by_far])
    other = jnp.stack([swap(mine), swap(by_near), swap(cross), swap(by_far)])
    both = jnp.stack([owned, other], axis=1)
    return both.reshape(-1, mine.shape[1])


def reduce_tokens(state, partial_value):
    tokens, width = state.shape
    blocks = partial_value.reshape(4, 2, tokens, width)
    half = tokens // 2
    arrived = swap(blocks[:, 1])
    total = blocks[:, 0] + arrived
    low = near(total[2, :half]).astype(jnp.float32)
    high = far(total[2, half:]).astype(jnp.float32)
    to_far = jnp.concatenate(
        [(total[3, :half].astype(jnp.float32) + low).astype(jnp.bfloat16), total[3, half:]]
    )
    to_near = jnp.concatenate(
        [total[1, :half], (total[1, half:].astype(jnp.float32) + high).astype(jnp.bfloat16)]
    )
    by_near, by_far = near(to_near), far(to_far)
    update = total[0].astype(jnp.float32) + by_near.astype(jnp.float32) + by_far.astype(jnp.float32)
    return (state.astype(jnp.float32) + update).astype(jnp.bfloat16)


def body(hidden, w_query, w_key, w_value, w_out, video_len, audio_len):
    batch = lax.axis_index("pipe")
    depth = lax.axis_index("z")
    ring = lax.axis_index("y")
    core = lax.axis_index("core")
    batches, tokens, width = hidden.shape
    features = w_query.shape[3]
    rows = w_query.shape[2]
    quarter = features // 4
    layers = 4
    factor = HEAD ** (-0.5)
    turned = jnp.transpose(w_out[0], (0, 2, 1))
    parts = jnp.stack([w_query[0], w_key[0], w_value[0], turned])
    parts = parts.reshape(4, 2, rows, 4, quarter).transpose(0, 3, 1, 2, 4)
    parts = parts.reshape(32, rows, quarter)
    moved = lax.all_to_all(parts, ("pipe", "y", "core"), 0, 0, tiled=True)
    moved = moved.reshape(layers, 8 * rows, quarter)
    gathered = [
        lax.all_gather(moved[layer], ("pipe", "z"), axis=0).reshape(4, width, quarter)
        for layer in range(layers)
    ]
    state = lax.dynamic_index_in_dim(hidden, batch, 0, keepdims=False)
    low, high = ring % 2, ring // 2
    lengths = jnp.where(core == 0, audio_len[batch], video_len[batch])
    flip = 2 * tokens * low + tokens * core
    ctl = jnp.stack(
        [flip, core, lengths[2 * depth + high], lengths[2 * depth + 1 - high]]
    ).astype(jnp.int32)
    for layer in range(layers):
        weights = gathered[layer]
        normed = gather_tokens(rms_norm(state))

        def project(index, scale):
            made = jnp.dot(normed, weights[index], preferred_element_type=jnp.float32)
            return (made * scale).astype(jnp.bfloat16)

        attended = attend(ctl, project(0, factor), project(1, 1.0), project(2, 1.0), tokens)
        partial_value = lax.dot_general(
            attended, weights[3], (((1,), (1,)), ((), ())), preferred_element_type=jnp.float32
        ).astype(jnp.bfloat16)
        state = reduce_tokens(state, partial_value)
    return state[None]


def solution(mesh):
    inner = Mesh(mesh.devices.reshape(4, 8, 4, 2), ("pipe", "z", "y", "core"))
    dp = ("z", "y", "core")
    return jax.shard_map(
        body,
        mesh=inner,
        in_specs=(
            P(None, dp, None),
            P("pipe", None, dp, None),
            P("pipe", None, dp, None),
            P("pipe", None, dp, None),
            P("pipe", None, None, dp),
            P(),
            P(),
        ),
        out_specs=P("pipe", dp, None),
        check_vma=False,
    )
```

time: 836 us -> 510 us (0.61)
  waiting for transfers between devices: 573 us -> 353 us
  matrix products: 88.9 us -> 27.7 us
  starting transfers between devices: 70.5 us -> 34 us
  other arithmetic: 33.1 us -> 9.36 us
  local copies, waits for them, and re-layouts: 43.8 us -> 24.1 us
  Pallas kernels: 0 us -> 15.4 us
  between operations: 1.53 us -> 14.1 us
    all_to_all x4 -> x0, waiting for transfers between devices: 380 us -> none  [the longest x1 106 us: body(): lax.all_to_all(spread_columns(w_query[0], count), 'dp', split_axis=1, con...]
    all_gather x0 -> x4, waiting for transfers between devices: none -> 259 us  [body(): lax.all_gather(moved[layer], ('pipe', 'z'), axis=0)]
    ppermute x34 -> x52, waiting for transfers between devices: 192 us -> 92.5 us  [the longest x16 45.6 us: far(): return lax.ppermute(value, 'y', FAR)]
    dot_general x77 -> x16, matrix products: 78.5 us -> 27.7 us  [the longest x12 19.9 us: project(): made = jnp.dot(normed, weights[index], preferred_element_type=jnp.float32)]
    all_to_all x4 -> x0, starting transfers between devices: 32 us -> none  [the longest x1 11.7 us: body(): lax.all_to_all(spread_columns(w_key[0], count), 'dp', split_axis=1, conca...]
    pallas_call x0 -> x4, Pallas kernels: none -> 15.4 us  [attend(): pl.pallas_call(functools.partial(attend_kernel, tokens=tokens), out_shape...]
    unnamed x96 -> x8, local copies, waits for them, and re-layouts: 13.9 us -> 0.04 us
    broadcast_in_dim x5 -> x0, local copies, waits for them, and re-layouts: 11.1 us -> none  [the longest x3 8.33 us: spread_columns(): jnp.broadcast_to(parts[:, None], (towers, count // 4, 4, rows, quarter))]
  transfers between devices with their start and end apart: 38 -> 56, of which waited for: 38 -> 34; matrix products, arithmetic and copies ran while one was open for 3% -> 9% of each run, Pallas kernels for 0% -> 2%
where the time goes in v1:
time: 510 us; the launch traced here: 502 us
  waiting for transfers between devices  353 us (69%)
  starting transfers between devices  34 us (7%)
  matrix products  27.7 us (5%)
  blocking collectives  24.5 us (5%)
  local copies, waits for them, and re-layouts  24.1 us (5%)
  Pallas kernels  15.4 us (3%)
  between operations  14.1 us (3%)
  other arithmetic  9.36 us (2%)
    all_gather x4, waiting for transfers between devices, body(): lax.all_gather(moved[layer], ('pipe', 'z'), axis=0)  259 us
    ppermute x16, waiting for transfers between devices, far(): return lax.ppermute(value, 'y', FAR)  45.6 us
    ppermute x16, waiting for transfers between devices, near(): return lax.ppermute(value, 'y', NEAR)  33 us
    all_to_all x1, blocking collectives, body(): moved = lax.all_to_all(parts, ('pipe', 'y', 'core'), 0, 0, tiled=True)  24.5 us
    ppermute x16, starting transfers between devices, far(): return lax.ppermute(value, 'y', FAR)  21.6 us
    dot_general x12, matrix products, project(): made = jnp.dot(normed, weights[index], preferred_element_type=jnp.float32)  19.9 us
    slice x4, local copies, waits for them, and re-layouts, body(): weights[3]  17.3 us
    pallas_call x4, Pallas kernels, attend(): pl.pallas_call(functools.partial(attend_kernel, tokens=tokens), out_shape...  15.4 us
  transfers between devices with their start and end apart: 56, of which 34 were waited for; matrix products, arithmetic and copies ran while one was open for 9% of the time, Pallas kernels for 2%

profile of v1, /device:TPU:56, one launch (start us, length us, event | category | flops | bytes accessed | tf_op | source)
XLA Modules:
  0.0 501.8 jit_solution(9262600020984501583)
XLA Ops:
  12.0 24.5 %all_to_all.5 = bf16[32,48,384]{2,1,0:T(8,128)(2,1)S(1)} all-to-all(bf16[32,48,384]{2,1,0:T(8,128)(2,1)S(1)} %bitcast.292), channel_id=1, replica_groups=mesh['pipe'=4,'z'=8,'y'=4,'core'=2] {'pipe','y','core'}, dimensions={0} | all-to-all | bytes 2359296 | tf_op jit(solution)/shard_map/all_to_all | solution.py:122
  43.0 4.6 collective-permute-done.1
  52.3 3.1 collective-permute-done.3
  58.6 81.0 %all-gather.5.cloned.1.call-done = bf16[32,384,384]{2,1,0:T(8,128)(2,1)} async-done(((bf16[1,384,384]{2,1,0:T(8,128)(2,1)}), bf16[32,384,384]{2,1,0:T(8,128)(2,1)}) %all-gather.5.cloned.1.call-update) | async-done | bytes 9437200 | tf_op jit(solution)/shard_map/all_gather | solution.py:125
  139.5 4.4 fusion.43
  148.9 3.8 shard_map.73
  154.9 2.3 collective-permute-done.8
  159.4 2.9 collective-permute-done.11
  165.5 4.4 collective-permute-done.10
  172.8 69.6 %all-gather.7.cloned.1.call-done = bf16[32,384,384]{2,1,0:T(8,128)(2,1)} async-done(((bf16[1,384,384]{2,1,0:T(8,128)(2,1)}), bf16[32,384,384]{2,1,0:T(8,128)(2,1)}) %all-gather.7.cloned.1.call-update) | async-done | bytes 9437200 | tf_op jit(solution)/shard_map/all_gather | solution.py:125
  242.4 4.3 fusion.42
  249.1 4.6 collective-permute-done.13
  255.3 4.4 collective-permute-done.16
  266.6 3.8 shard_map.74
  275.6 5.6 %collective-permute-done.22 = bf16[16,3072]{1,0:T(8,128)(2,1)S(1)} collective-permute-done((bf16[16,3072]{1,0:T(8,128)(2,1)S(1)}, bf16[16,3072]{1,0:T(8,128)(2,1)S(1)}, u32[]{:S(2)}, u32[]{:S(2)}) %collective-permute-start.22) | collective-permute-done | bytes 98336 | tf_op jit(solution)/shard_map/ppermute | solution.py:28
  283.4 4.0 collective-permute-done.23
  291.0 54.2 %all-gather.9.cloned.1.call-done = bf16[32,384,384]{2,1,0:T(8,128)(2,1)} async-done(((bf16[1,384,384]{2,1,0:T(8,128)(2,1)}), bf16[32,384,384]{2,1,0:T(8,128)(2,1)}) %all-gather.9.cloned.1.call-update) | async-done | bytes 9437200 | tf_op jit(solution)/shard_map/all_gather | solution.py:125
  345.3 4.3 fusion.41
  352.0 4.6 collective-permute-done.26
  357.9 4.8 collective-permute-done.29
  369.6 3.8 shard_map.75
  375.7 2.1 collective-permute-done.34
  378.6 5.6 %collective-permute-done.35 = bf16[16,3072]{1,0:T(8,128)(2,1)S(1)} collective-permute-done((bf16[16,3072]{1,0:T(8,128)(2,1)S(1)}, bf16[16,3072]{1,0:T(8,128)(2,1)S(1)}, u32[]{:S(2)}, u32[]{:S(2)}) %collective-permute-start.35) | collective-permute-done | bytes 98336 | tf_op jit(solution)/shard_map/ppermute | solution.py:28
  386.4 4.0 collective-permute-done.36
  394.0 54.0 %all-gather.11.cloned.1.call-done = bf16[32,384,384]{2,1,0:T(8,128)(2,1)} async-done(((bf16[1,384,384]{2,1,0:T(8,128)(2,1)}), bf16[32,384,384]{2,1,0:T(8,128)(2,1)}) %all-gather.11.cloned.1.call-update) | async-done | bytes 9437200 | tf_op jit(solution)/shard_map/all_gather | solution.py:125
  447.9 4.3 fusion.40
  454.9 4.4 collective-permute-done.39
  460.4 4.8 collective-permute-done.42
  472.1 3.8 shard_map.76
  478.2 2.1 collective-permute-done.47
  481.1 5.5 %collective-permute-done.48 = bf16[16,3072]{1,0:T(8,128)(2,1)S(1)} collective-permute-done((bf16[16,3072]{1,0:T(8,128)(2,1)S(1)}, bf16[16,3072]{1,0:T(8,128)(2,1)S(1)}, u32[]{:S(2)}, u32[]{:S(2)}) %collective-permute-start.48) | collective-permute-done | bytes 98336 | tf_op jit(solution)/shard_map/ppermute | solution.py:28
  488.9 4.0 collective-permute-done.49
  (195 shorter events, 93.8 us)
Async XLA Ops:
  6.5 133.0 %all-gather.5.cloned.1.call-start = ((), (), s32[]{:S(2)}) async-start(), calls=%async_computation.1 | async-start | bytes 9732096 | tf_op jit(solution)/shard_map/all_gather | solution.py:125
  37.5 204.9 %all-gather.7.cloned.1.call-start = ((), (), s32[]{:S(2)}) async-start(), calls=%async_computation.2 | async-start | bytes 9732096 | tf_op jit(solution)/shard_map/all_gather | solution.py:125
  38.3 307.0 %all-gather.9.cloned.1.call-start = ((), (), s32[]{:S(2)}) async-start(), calls=%async_computation.3 | async-start | bytes 9732096 | tf_op jit(solution)/shard_map/all_gather | solution.py:125
  39.0 408.9 %all-gather.11.cloned.1.call-start = ((), (), s32[]{:S(2)}) async-start(), calls=%async_computation.4 | async-start | bytes 9732096 | tf_op jit(solution)/shard_map/all_gather | solution.py:125
  39.4 8.2 %collective-permute-start.1 = (bf16[32,3072]{1,0:T(8,128)(2,1)S(1)}, bf16[32,3072]{1,0:T(8,128)(2,1)S(1)}, u32[]{:S(2)}, u32[]{:S(2)}) collective-permute-start(bf16[32,3072]{1,0:T(8,128)(2,1)S(1)} %fusion.12), channel_id=1, source_target_pairs={{2,4},{4,2},{6,0},{0,6},{3,5},{5,3},{7,1},{1,7},{10,12},{12,10},{1... | collective-permute-start | bytes 589832 | tf_op jit(solution)/shard_map/ppermute | solution.py:28
  41.5 8.0 %collective-permute-start = (bf16[32,3072]{1,0:T(8,128)(2,1)S(1)}, bf16[32,3072]{1,0:T(8,128)(2,1)S(1)}, u32[]{:S(2)}, u32[]{:S(2)}) collective-permute-start(bf16[32,3072]{1,0:T(8,128)(2,1)S(1)} %fusion.12), channel_id=1, source_target_pairs={{0,2},{2,0},{4,6},{6,4},{1,3},{3,1},{5,7},{7,5},{8,10},{10,8},{12,... | collective-permute-start | bytes 589832 | tf_op jit(solution)/shard_map/ppermute | solution.py:24
  41.5 14.3 %collective-permute-start.4 = (bf16[32,3072]{1,0:T(8,128)(2,1)S(1)}, bf16[32,3072]{1,0:T(8,128)(2,1)S(1)}, u32[]{:S(2)}, u32[]{:S(2)}) collective-permute-start(bf16[32,3072]{1,0:T(8,128)(2,1)S(1)} %fusion.12), channel_id=1, source_target_pairs={{0,1},{1,0},{2,3},{3,2},{4,5},{5,4},{6,7},{7,6},{8,9},{9,8},{10,11... | collective-permute-start | bytes 589832 | tf_op jit(solution)/shard_map/ppermute | solution.py:32
  49.5 5.9 %collective-permute-start.3 = (bf16[16,3072]{1,0:T(8,128)(2,1)S(1)}, bf16[16,3072]{1,0:T(8,128)(2,1)S(1)}, u32[]{:S(2)}, u32[]{:S(2)}) collective-permute-start(bf16[16,3072]{1,0:T(8,128)(2,1)S(1)} %slice.289), channel_id=1, source_target_pairs={{2,4},{4,2},{6,0},{0,6},{3,5},{5,3},{7,1},{1,7},{10,12},{12,10},{1... | collective-permute-start | bytes 294920 | tf_op jit(solution)/shard_map/ppermute | solution.py:28
  164.2 7.0 %collective-permute-start.12 = (bf16[32,3072]{1,0:T(8,128)(2,1)S(1)}, bf16[32,3072]{1,0:T(8,128)(2,1)S(1)}, u32[]{:S(2)}, u32[]{:S(2)}) collective-permute-start(bf16[32,3072]{1,0:T(8,128)(2,1)S(1)} %pad_maximum_fusion.5), channel_id=1, source_target_pairs={{2,4},{4,2},{6,0},{0,6},{3,5},{5,3},{7,1},{1,7},{10,12},{12,10},{1... | collective-permute-start | bytes 589832 | tf_op jit(solution)/shard_map/ppermute | solution.py:28
  171.6 76.1 %collective-permute-start.14 = (bf16[32,3072]{1,0:T(8,128)(2,1)S(1)}, bf16[32,3072]{1,0:T(8,128)(2,1)S(1)}, u32[]{:S(2)}, u32[]{:S(2)}) collective-permute-start(bf16[32,3072]{1,0:T(8,128)(2,1)S(1)} %fusion.16), channel_id=1, source_target_pairs={{2,4},{4,2},{6,0},{0,6},{3,5},{5,3},{7,1},{1,7},{10,12},{12,10},{1... | collective-permute-start | bytes 589832 | tf_op jit(solution)/shard_map/ppermute | solution.py:28
  246.7 7.1 %collective-permute-start.13 = (bf16[32,3072]{1,0:T(8,128)(2,1)S(1)}, bf16[32,3072]{1,0:T(8,128)(2,1)S(1)}, u32[]{:S(2)}, u32[]{:S(2)}) collective-permute-start(bf16[32,3072]{1,0:T(8,128)(2,1)S(1)} %fusion.16), channel_id=1, source_target_pairs={{0,2},{2,0},{4,6},{6,4},{1,3},{3,1},{5,7},{7,5},{8,10},{10,8},{12,... | collective-permute-start | bytes 589832 | tf_op jit(solution)/shard_map/ppermute | solution.py:24
  247.7 7.6 %collective-permute-start.15 = (bf16[16,3072]{1,0:T(8,128)(2,1)S(1)}, bf16[16,3072]{1,0:T(8,128)(2,1)S(1)}, u32[]{:S(2)}, u32[]{:S(2)}) collective-permute-start(bf16[16,3072]{1,0:T(8,128)(2,1)S(1)} %slice.304), channel_id=1, source_target_pairs={{0,2},{2,0},{4,6},{6,4},{1,3},{3,1},{5,7},{7,5},{8,10},{10,8},{12,... | collective-permute-start | bytes 294920 | tf_op jit(solution)/shard_map/ppermute | solution.py:24
  249.0 10.9 %collective-permute-start.17 = (bf16[32,3072]{1,0:T(8,128)(2,1)S(1)}, bf16[32,3072]{1,0:T(8,128)(2,1)S(1)}, u32[]{:S(2)}, u32[]{:S(2)}) collective-permute-start(bf16[32,3072]{1,0:T(8,128)(2,1)S(1)} %fusion.16), channel_id=1, source_target_pairs={{0,1},{1,0},{2,3},{3,2},{4,5},{5,4},{6,7},{7,6},{8,9},{9,8},{10,11... | collective-permute-start | bytes 589832 | tf_op jit(solution)/shard_map/ppermute | solution.py:32
  275.0 6.2 %collective-permute-start.22 = (bf16[16,3072]{1,0:T(8,128)(2,1)S(1)}, bf16[16,3072]{1,0:T(8,128)(2,1)S(1)}, u32[]{:S(2)}, u32[]{:S(2)}) collective-permute-start(bf16[16,3072]{1,0:T(8,128)(2,1)S(1)} %get-tuple-element.46), channel_id=1, source_target_pairs={{2,4},{4,2},{6,0},{0,6},{3,5},{5,3},{7,1},{1,7},{10,12},{12,10},{1... | collective-permute-start | bytes 294920 | tf_op jit(solution)/shard_map/ppermute | solution.py:28
  281.2 6.2 %collective-permute-start.23 = (bf16[32,3072]{1,0:T(8,128)(2,1)S(1)}, bf16[32,3072]{1,0:T(8,128)(2,1)S(1)}, u32[]{:S(2)}, u32[]{:S(2)}) collective-permute-start(bf16[32,3072]{1,0:T(8,128)(2,1)S(1)} %pad_maximum_fusion.6), channel_id=1, source_target_pairs={{0,2},{2,0},{4,6},{6,4},{1,3},{3,1},{5,7},{7,5},{8,10},{10,8},{12,... | collective-permute-start | bytes 589832 | tf_op jit(solution)/shard_map/ppermute | solution.py:24
  281.3 7.4 %collective-permute-start.25 = (bf16[32,3072]{1,0:T(8,128)(2,1)S(1)}, bf16[32,3072]{1,0:T(8,128)(2,1)S(1)}, u32[]{:S(2)}, u32[]{:S(2)}) collective-permute-start(bf16[32,3072]{1,0:T(8,128)(2,1)S(1)} %pad_maximum_fusion.7), channel_id=1, source_target_pairs={{2,4},{4,2},{6,0},{0,6},{3,5},{5,3},{7,1},{1,7},{10,12},{12,10},{1... | collective-permute-start | bytes 589832 | tf_op jit(solution)/shard_map/ppermute | solution.py:28
  289.1 61.4 %collective-permute-start.27 = (bf16[32,3072]{1,0:T(8,128)(2,1)S(1)}, bf16[32,3072]{1,0:T(8,128)(2,1)S(1)}, u32[]{:S(2)}, u32[]{:S(2)}) collective-permute-start(bf16[32,3072]{1,0:T(8,128)(2,1)S(1)} %fusion.19), channel_id=1, source_target_pairs={{2,4},{4,2},{6,0},{0,6},{3,5},{5,3},{7,1},{1,7},{10,12},{12,10},{1... | collective-permute-start | bytes 589832 | tf_op jit(solution)/shard_map/ppermute | solution.py:28
  349.6 7.1 %collective-permute-start.26 = (bf16[32,3072]{1,0:T(8,128)(2,1)S(1)}, bf16[32,3072]{1,0:T(8,128)(2,1)S(1)}, u32[]{:S(2)}, u32[]{:S(2)}) collective-permute-start(bf16[32,3072]{1,0:T(8,128)(2,1)S(1)} %fusion.19), channel_id=1, source_target_pairs={{0,2},{2,0},{4,6},{6,4},{1,3},{3,1},{5,7},{7,5},{8,10},{10,8},{12,... | collective-permute-start | bytes 589832 | tf_op jit(solution)/shard_map/ppermute | solution.py:24
  350.5 7.4 %collective-permute-start.28 = (bf16[16,3072]{1,0:T(8,128)(2,1)S(1)}, bf16[16,3072]{1,0:T(8,128)(2,1)S(1)}, u32[]{:S(2)}, u32[]{:S(2)}) collective-permute-start(bf16[16,3072]{1,0:T(8,128)(2,1)S(1)} %slice.320), channel_id=1, source_target_pairs={{0,2},{2,0},{4,6},{6,4},{1,3},{3,1},{5,7},{7,5},{8,10},{10,8},{12,... | collective-permute-start | bytes 294920 | tf_op jit(solution)/shard_map/ppermute | solution.py:24
  351.9 11.1 %collective-permute-start.30 = (bf16[32,3072]{1,0:T(8,128)(2,1)S(1)}, bf16[32,3072]{1,0:T(8,128)(2,1)S(1)}, u32[]{:S(2)}, u32[]{:S(2)}) collective-permute-start(bf16[32,3072]{1,0:T(8,128)(2,1)S(1)} %fusion.19), channel_id=1, source_target_pairs={{0,1},{1,0},{2,3},{3,2},{4,5},{5,4},{6,7},{7,6},{8,9},{9,8},{10,11... | collective-permute-start | bytes 589832 | tf_op jit(solution)/shard_map/ppermute | solution.py:32
  356.6 6.1 %collective-permute-start.29 = (bf16[16,3072]{1,0:T(8,128)(2,1)S(1)}, bf16[16,3072]{1,0:T(8,128)(2,1)S(1)}, u32[]{:S(2)}, u32[]{:S(2)}) collective-permute-start(bf16[16,3072]{1,0:T(8,128)(2,1)S(1)} %slice.321), channel_id=1, source_target_pairs={{2,4},{4,2},{6,0},{0,6},{3,5},{5,3},{7,1},{1,7},{10,12},{12,10},{1... | collective-permute-start | bytes 294920 | tf_op jit(solution)/shard_map/ppermute | solution.py:28
  378.0 6.1 %collective-permute-start.35 = (bf16[16,3072]{1,0:T(8,128)(2,1)S(1)}, bf16[16,3072]{1,0:T(8,128)(2,1)S(1)}, u32[]{:S(2)}, u32[]{:S(2)}) collective-permute-start(bf16[16,3072]{1,0:T(8,128)(2,1)S(1)} %get-tuple-element.40), channel_id=1, source_target_pairs={{2,4},{4,2},{6,0},{0,6},{3,5},{5,3},{7,1},{1,7},{10,12},{12,10},{1... | collective-permute-start | bytes 294920 | tf_op jit(solution)/shard_map/ppermute | solution.py:28
  384.2 6.2 %collective-permute-start.36 = (bf16[32,3072]{1,0:T(8,128)(2,1)S(1)}, bf16[32,3072]{1,0:T(8,128)(2,1)S(1)}, u32[]{:S(2)}, u32[]{:S(2)}) collective-permute-start(bf16[32,3072]{1,0:T(8,128)(2,1)S(1)} %pad_maximum_fusion.8), channel_id=1, source_target_pairs={{0,2},{2,0},{4,6},{6,4},{1,3},{3,1},{5,7},{7,5},{8,10},{10,8},{12,... | collective-permute-start | bytes 589832 | tf_op jit(solution)/shard_map/ppermute | solution.py:24
  384.3 7.4 %collective-permute-start.38 = (bf16[32,3072]{1,0:T(8,128)(2,1)S(1)}, bf16[32,3072]{1,0:T(8,128)(2,1)S(1)}, u32[]{:S(2)}, u32[]{:S(2)}) collective-permute-start(bf16[32,3072]{1,0:T(8,128)(2,1)S(1)} %pad_maximum_fusion.9), channel_id=1, source_target_pairs={{2,4},{4,2},{6,0},{0,6},{3,5},{5,3},{7,1},{1,7},{10,12},{12,10},{1... | collective-permute-start | bytes 589832 | tf_op jit(solution)/shard_map/ppermute | solution.py:28
  392.1 61.1 %collective-permute-start.40 = (bf16[32,3072]{1,0:T(8,128)(2,1)S(1)}, bf16[32,3072]{1,0:T(8,128)(2,1)S(1)}, u32[]{:S(2)}, u32[]{:S(2)}) collective-permute-start(bf16[32,3072]{1,0:T(8,128)(2,1)S(1)} %fusion.22), channel_id=1, source_target_pairs={{2,4},{4,2},{6,0},{0,6},{3,5},{5,3},{7,1},{1,7},{10,12},{12,10},{1... | collective-permute-start | bytes 589832 | tf_op jit(solution)/shard_map/ppermute | solution.py:28
  452.3 7.1 %collective-permute-start.39 = (bf16[32,3072]{1,0:T(8,128)(2,1)S(1)}, bf16[32,3072]{1,0:T(8,128)(2,1)S(1)}, u32[]{:S(2)}, u32[]{:S(2)}) collective-permute-start(bf16[32,3072]{1,0:T(8,128)(2,1)S(1)} %fusion.22), channel_id=1, source_target_pairs={{0,2},{2,0},{4,6},{6,4},{1,3},{3,1},{5,7},{7,5},{8,10},{10,8},{12,... | collective-permute-start | bytes 589832 | tf_op jit(solution)/shard_map/ppermute | solution.py:24
  453.2 7.2 %collective-permute-start.41 = (bf16[16,3072]{1,0:T(8,128)(2,1)S(1)}, bf16[16,3072]{1,0:T(8,128)(2,1)S(1)}, u32[]{:S(2)}, u32[]{:S(2)}) collective-permute-start(bf16[16,3072]{1,0:T(8,128)(2,1)S(1)} %slice.336), channel_id=1, source_target_pairs={{0,2},{2,0},{4,6},{6,4},{1,3},{3,1},{5,7},{7,5},{8,10},{10,8},{12,... | collective-permute-start | bytes 294920 | tf_op jit(solution)/shard_map/ppermute | solution.py:24
  454.6 10.9 %collective-permute-start.43 = (bf16[32,3072]{1,0:T(8,128)(2,1)S(1)}, bf16[32,3072]{1,0:T(8,128)(2,1)S(1)}, u32[]{:S(2)}, u32[]{:S(2)}) collective-permute-start(bf16[32,3072]{1,0:T(8,128)(2,1)S(1)} %fusion.22), channel_id=1, source_target_pairs={{0,1},{1,0},{2,3},{3,2},{4,5},{5,4},{6,7},{7,6},{8,9},{9,8},{10,11... | collective-permute-start | bytes 589832 | tf_op jit(solution)/shard_map/ppermute | solution.py:32
  459.3 5.9 %collective-permute-start.42 = (bf16[16,3072]{1,0:T(8,128)(2,1)S(1)}, bf16[16,3072]{1,0:T(8,128)(2,1)S(1)}, u32[]{:S(2)}, u32[]{:S(2)}) collective-permute-start(bf16[16,3072]{1,0:T(8,128)(2,1)S(1)} %slice.337), channel_id=1, source_target_pairs={{2,4},{4,2},{6,0},{0,6},{3,5},{5,3},{7,1},{1,7},{10,12},{12,10},{1... | collective-permute-start | bytes 294920 | tf_op jit(solution)/shard_map/ppermute | solution.py:28
  480.5 6.1 %collective-permute-start.48 = (bf16[16,3072]{1,0:T(8,128)(2,1)S(1)}, bf16[16,3072]{1,0:T(8,128)(2,1)S(1)}, u32[]{:S(2)}, u32[]{:S(2)}) collective-permute-start(bf16[16,3072]{1,0:T(8,128)(2,1)S(1)} %get-tuple-element.34), channel_id=1, source_target_pairs={{2,4},{4,2},{6,0},{0,6},{3,5},{5,3},{7,1},{1,7},{10,12},{12,10},{1... | collective-permute-start | bytes 294920 | tf_op jit(solution)/shard_map/ppermute | solution.py:28
  486.7 6.2 %collective-permute-start.49 = (bf16[32,3072]{1,0:T(8,128)(2,1)S(1)}, bf16[32,3072]{1,0:T(8,128)(2,1)S(1)}, u32[]{:S(2)}, u32[]{:S(2)}) collective-permute-start(bf16[32,3072]{1,0:T(8,128)(2,1)S(1)} %pad_maximum_fusion.10), channel_id=1, source_target_pairs={{0,2},{2,0},{4,6},{6,4},{1,3},{3,1},{5,7},{7,5},{8,10},{10,8},{12,... | collective-permute-start | bytes 589832 | tf_op jit(solution)/shard_map/ppermute | solution.py:24
  486.8 7.4 %collective-permute-start.51 = (bf16[32,3072]{1,0:T(8,128)(2,1)S(1)}, bf16[32,3072]{1,0:T(8,128)(2,1)S(1)}, u32[]{:S(2)}, u32[]{:S(2)}) collective-permute-start(bf16[32,3072]{1,0:T(8,128)(2,1)S(1)} %pad_maximum_fusion.11), channel_id=1, source_target_pairs={{2,4},{4,2},{6,0},{0,6},{3,5},{5,3},{7,1},{1,7},{10,12},{12,10},{1... | collective-permute-start | bytes 589832 | tf_op jit(solution)/shard_map/ppermute | solution.py:28
  (26 other events, 132.6 us)
Sparse Core Ops, SparseCore 0:
  37.7 101.8 all-gather.4
  142.1 100.2 all-gather.6
  245.0 100.2 all-gather.8
  347.7 100.2 all-gather.10

commit v2 on v1

v2 whole, which is shorter than its diff:
```python
import functools

import jax
import jax.numpy as jnp
from jax import lax
from jax.experimental import pallas as pl
from jax.experimental.pallas import tpu as pltpu
from jax.sharding import Mesh
from jax.sharding import PartitionSpec as P

HEAD = 128
NEAR = [(0, 1), (1, 0), (2, 3), (3, 2)]
FAR = [(1, 2), (2, 1), (3, 0), (0, 3)]
SWAP = [(0, 1), (1, 0)]


def rms_norm(values):
    wide = values.astype(jnp.float32)
    scale = lax.rsqrt(jnp.mean(wide * wide, axis=-1, keepdims=True) + 1e-06)
    return (wide * scale).astype(jnp.bfloat16)


def near(value):
    return lax.ppermute(value, "y", NEAR)


def far(value):
    return lax.ppermute(value, "y", FAR)


def swap(value):
    return lax.ppermute(value, "core", SWAP)


OFFSETS = (0, 7, 6, 5, 1, 2, 3, 4)


def block_kernel(ctl, *refs, tokens, along_depth, pieces):
    mine, by_near, by_far, cross, swapped, swapped_cross = refs[:6]
    weights = refs[6 : 6 + pieces]
    keep, give, held, normed, sums, mixed_all, sems = refs[6 + pieces :]
    size = held.shape[2]
    copies = []
    if along_depth:
        for slot in range(7):
            copies.append([pltpu.make_async_copy(weights[slot], held.at[slot], sems.at[slot])])
        copies.append(
            [
                pltpu.make_async_copy(weights[7], held.at[7, 0:2], sems.at[7]),
                pltpu.make_async_copy(weights[8], held.at[7, 2:4], sems.at[8]),
            ]
        )
    else:
        for slot, source in ((0, 0), (1, 1), (3, 2)):
            copies.append([pltpu.make_async_copy(weights[source], held.at[slot], sems.at[slot])])
        copies.insert(
            2,
            [
                pltpu.make_async_copy(weights[3], held.at[2, 0:4], sems.at[2]),
                pltpu.make_async_copy(weights[4], held.at[2, 4:8], sems.at[4]),
            ],
        )
    for group in copies:
        for copy in group:
            copy.start()
    flip, core, section, depth = ctl[0], ctl[1], ctl[4], ctl[5]
    for block, (own, other) in enumerate(
        ((mine, swapped.at[0]), (by_near, swapped.at[1]), (cross, swapped_cross), (by_far, swapped.at[2]))
    ):
        normed[pl.ds(2 * block * tokens, tokens), :] = own[...]
        normed[pl.ds((2 * block + 1) * tokens, tokens), :] = other[...]
    sums[...] = jnp.zeros_like(sums)

    def columns(slot):
        place = (depth + ctl[8 + slot]) & 7
        return pl.ds(pl.multiple_of(place * size, 128), size)

    def add(outer, inner):
        index, slot = (inner, outer) if along_depth else (outer, inner)
        array = section ^ index

        @pl.when(array != 3)
        def _():
            sums[array] += jnp.dot(
                normed[:, columns(slot)], held[outer, inner], preferred_element_type=jnp.float32
            )

    for outer, group in enumerate(copies):
        for copy in group:
            copy.wait()
        pl.loop(0, held.shape[1])(functools.partial(add, outer))

    rows = 4 * tokens
    heads = size // HEAD
    key_place = lax.broadcasted_iota(jnp.int32, (rows, rows), 1) ^ flip
    query_place = lax.broadcasted_iota(jnp.int32, (rows, HEAD), 0) ^ flip
    video = 3 * tokens
    first = jnp.where(core == 0, video, 0)
    own_low = jnp.where(core == 0, 0, video)
    own_high = jnp.where(core == 0, video, rows)
    live = (query_place >= own_low) & (query_place < own_high)
    for sample in range(2):
        valid = (key_place >= first) & (key_place < first + ctl[2 + sample])
        span = pl.ds(sample * rows, rows)
        for head in range(heads):
            cols = pl.ds(head * HEAD, HEAD)
            scores = lax.dot_general(
                (sums[0, span, cols] * HEAD ** (-0.5)).astype(jnp.bfloat16),
                sums[1, span, cols].astype(jnp.bfloat16),
                (((1,), (1,)), ((), ())),
                preferred_element_type=jnp.float32,
            )
            scores = jnp.where(valid, scores, -1e30)
            top = jnp.max(scores, axis=-1, keepdims=True)
            powers = jnp.exp(scores - top)
            shares = (powers / jnp.sum(powers, axis=-1, keepdims=True)).astype(jnp.bfloat16)
            mixed = jnp.dot(
                shares, sums[2, span, cols].astype(jnp.bfloat16), preferred_element_type=jnp.float32
            )
            mixed_all[span, cols] = jnp.where(live, mixed, 0.0).astype(jnp.bfloat16)
    last = section ^ 3

    @pl.loop(0, 8)
    def _(slot):
        piece = held[slot, last] if along_depth else held[last, slot]
        made = lax.dot_general(
            mixed_all[...], piece, (((1,), (1,)), ((), ())), preferred_element_type=jnp.float32
        ).astype(jnp.bfloat16)
        for block in range(4):
            keep[block, :, columns(slot)] = made[2 * block * tokens : (2 * block + 1) * tokens]
            give[block, :, columns(slot)] = made[(2 * block + 1) * tokens : (2 * block + 2) * tokens]


def run_block(ctl, blocks, weights, tokens, width, along_depth):
    size = weights[0].shape[1]
    vmem = pl.BlockSpec(memory_space=pltpu.VMEM)
    there = pl.BlockSpec(memory_space=pl.ANY)
    shape = (8, 4, size, size) if along_depth else (4, 8, size, size)
    out = jax.ShapeDtypeStruct((4, tokens, width), jnp.bfloat16)
    count = 8 * tokens
    return pl.pallas_call(
        functools.partial(
            block_kernel, tokens=tokens, along_depth=along_depth, pieces=len(weights)
        ),
        out_shape=(out, out),
        in_specs=[pl.BlockSpec(memory_space=pltpu.SMEM)] + [vmem] * 6 + [there] * len(weights),
        out_specs=(vmem, vmem),
        scratch_shapes=[
            pltpu.VMEM(shape, jnp.bfloat16),
            pltpu.VMEM((count, width), jnp.bfloat16),
            pltpu.VMEM((3, count, size), jnp.float32),
            pltpu.VMEM((count, size), jnp.bfloat16),
            pltpu.SemaphoreType.DMA((9,)),
        ],
        compiler_params=pltpu.CompilerParams(vmem_limit_bytes=24 << 20),
        cost_estimate=pl.CostEstimate(
            flops=8 * count * width * size,
            bytes_accessed=8 * width * size + 6 * count * width,
            transcendentals=count * size,
        ),
    )(ctl, *blocks, *weights)


def gather_tokens(mine):
    by_near, by_far = near(mine), far(mine)
    cross = near(by_far)
    return mine, by_near, by_far, cross, swap(jnp.stack([mine, by_near, by_far])), swap(cross)


def reduce_tokens(state, keep, give):
    total = keep + swap(give)
    passed = near(total[2])
    by_near = near(total[1])
    to_far = (total[3].astype(jnp.float32) + passed.astype(jnp.float32)).astype(jnp.bfloat16)
    by_far = far(to_far)
    update = total[0].astype(jnp.float32) + by_near.astype(jnp.float32) + by_far.astype(jnp.float32)
    return (state.astype(jnp.float32) + update).astype(jnp.bfloat16)


def up(value):
    return lax.ppermute(value, "z", [(place, (place + 1) % 8) for place in range(8)])


def down(value):
    return lax.ppermute(value, "z", [(place, (place - 1) % 8) for place in range(8)])


def beside(value):
    return lax.ppermute(value, "pipe", NEAR)


def around(value):
    return lax.ppermute(value, "pipe", FAR)


def spread_across_then_deep(shard):
    by_beside, by_around = beside(shard), around(shard)
    four = jnp.stack([shard, by_beside, beside(by_around), by_around])
    below = [up(four)]
    above = [down(four)]
    for _ in range(2):
        below.append(up(below[-1]))
        above.append(down(above[-1]))
    return [four, *below, *above, up(below[-1][:2]), down(above[-1][2:])]


def spread_deep_then_across(shard):
    below = [up(shard)]
    above = [down(shard)]
    for _ in range(2):
        below.append(up(below[-1]))
        above.append(down(above[-1]))
    eight = jnp.stack([shard, *below, *above, down(above[-1])])
    by_beside, by_around = beside(eight), around(eight)
    return [eight, by_beside, by_around, beside(by_around[:4]), around(by_beside[4:])]


def body(hidden, w_query, w_key, w_value, w_out, video_len, audio_len):
    batch = lax.axis_index("pipe")
    depth = lax.axis_index("z")
    ring = lax.axis_index("y")
    core = lax.axis_index("core")
    batches, tokens, width = hidden.shape
    features = w_query.shape[3]
    rows = w_query.shape[2]
    quarter = features // 4
    layers = 4
    turned = jnp.transpose(w_out[0], (0, 2, 1))
    parts = jnp.stack([w_query[0], w_key[0], w_value[0], turned])
    parts = parts.reshape(4, 2, rows, 4, quarter).transpose(0, 3, 1, 2, 4)
    parts = parts.reshape(32, rows, quarter)
    moved = lax.all_to_all(parts, ("pipe", "y", "core"), 0, 0, tiled=True)
    moved = moved.reshape(layers, 8 * rows, quarter)
    gathered = [
        (spread_deep_then_across if layer % 2 else spread_across_then_deep)(moved[layer])
        for layer in range(layers)
    ]
    state = lax.dynamic_index_in_dim(hidden, batch, 0, keepdims=False)
    low, high = ring % 2, ring // 2
    lengths = jnp.where(core == 0, audio_len[batch], video_len[batch])
    flip = 2 * tokens * low + tokens * core
    zero = jnp.int32(0)
    ctl = jnp.stack(
        [flip, core, lengths[2 * depth + high], lengths[2 * depth + 1 - high], batch, depth, zero, zero]
        + [jnp.int32(step) for step in OFFSETS]
    ).astype(jnp.int32)
    for layer in range(layers):
        blocks = gather_tokens(rms_norm(state))
        keep, give = run_block(ctl, blocks, gathered[layer], tokens, width, layer % 2 == 0)
        state = reduce_tokens(state, keep, give)
    return state[None]


def solution(mesh):
    inner = Mesh(mesh.devices.reshape(4, 8, 4, 2), ("pipe", "z", "y", "core"))
    dp = ("z", "y", "core")
    return jax.shard_map(
        body,
        mesh=inner,
        in_specs=(
            P(None, dp, None),
            P("pipe", None, dp, None),
            P("pipe", None, dp, None),
            P("pipe", None, dp, None),
            P("pipe", None, None, dp),
            P(),
            P(),
        ),
        out_specs=P("pipe", dp, None),
        check_vma=False,
    )
```

time: 510 us -> 538 us (1.055)
  starting transfers between devices: 34 us -> 93.5 us
  Pallas kernels: 15.4 us -> 53.5 us
  matrix products: 27.7 us -> 0 us
  waiting for transfers between devices: 353 us -> 331 us
  between operations: 14.1 us -> 1.11 us
  local copies, waits for them, and re-layouts: 24.1 us -> 11.6 us
    ppermute x0 -> x44, waiting for transfers between devices: none -> 272 us  [the longest x6 104 us: around(): return lax.ppermute(value, 'pipe', FAR)]
    all_gather x4 -> x0, waiting for transfers between devices: 259 us -> none  [body(): lax.all_gather(moved[layer], ('pipe', 'z'), axis=0)]
    ppermute x0 -> x44, starting transfers between devices: none -> 57.5 us  [the longest x16 33.7 us: down(): lax.ppermute(value, 'z', [(place, (place - 1) % 8) for place in range(8)])]
    pallas_call x4, Pallas kernels: 15.4 us -> 53.5 us  [run_block(): pl.pallas_call(functools.partial(block_kernel, tokens=tokens, along_depth...]
    ppermute x16 -> x8, waiting for transfers between devices: 45.6 us -> 12.4 us  [far(): return lax.ppermute(value, 'y', FAR)]
    dot_general x16 -> x0, matrix products: 27.7 us -> none  [the longest x12 19.9 us: project(): made = jnp.dot(normed, weights[index], preferred_element_type=jnp.float32)]
    slice x12 -> x8, local copies, waits for them, and re-layouts: 17.4 us -> 0.72 us  [the longest x4 0.24 us: spread_across_then_deep(): return [four, *below, *above, up(below[-1][:2]), down(above[-1][2:])]]
    ppermute x16, starting transfers between devices: 7.99 us -> 18.1 us  [near(): return lax.ppermute(value, 'y', NEAR)]
  transfers between devices with their start and end apart: 56 -> 80, of which waited for: 34 -> 39; matrix products, arithmetic and copies ran while one was open for 9% -> 3% of each run, Pallas kernels for 2% -> 8%
where the time goes in v2:
time: 538 us; the launch traced here: 527 us
  waiting for transfers between devices  331 us (62%)
  starting transfers between devices  93.5 us (17%)
  Pallas kernels  53.5 us (10%)
  blocking collectives  24.4 us (5%)
  other arithmetic  12 us (2%)
  local copies, waits for them, and re-layouts  11.6 us (2%)
    ppermute x6, waiting for transfers between devices, around(): return lax.ppermute(value, 'pipe', FAR)  104 us
    ppermute x14, waiting for transfers between devices, up(): lax.ppermute(value, 'z', [(place, (place + 1) % 8) for place in range(8)])  102 us
    pallas_call x4, Pallas kernels, run_block(): pl.pallas_call(functools.partial(block_kernel, tokens=tokens, along_depth...  53.5 us
    ppermute x16, waiting for transfers between devices, near(): return lax.ppermute(value, 'y', NEAR)  41.5 us
    ppermute x16, waiting for transfers between devices, down(): lax.ppermute(value, 'z', [(place, (place - 1) % 8) for place in range(8)])  38.2 us
    ppermute x16, starting transfers between devices, down(): lax.ppermute(value, 'z', [(place, (place - 1) % 8) for place in range(8)])  33.7 us
    ppermute x8, waiting for transfers between devices, beside(): return lax.ppermute(value, 'pipe', NEAR)  27.6 us
    all_to_all x1, blocking collectives, body(): moved = lax.all_to_all(parts, ('pipe', 'y', 'core'), 0, 0, tiled=True)  24.4 us
  transfers between devices with their start and end apart: 80, of which 39 were waited for; matrix products, arithmetic and copies ran while one was open for 3% of the time, Pallas kernels for 8%

profile of v2, /device:TPU:56, one launch (start us, length us, event | category | flops | bytes accessed | tf_op | source)
XLA Modules:
  0.0 527.4 jit_solution(13215181602752083809)
XLA Ops:
  5.4 24.4 %all_to_all.5 = bf16[32,48,384]{2,1,0:T(8,128)(2,1)S(1)} all-to-all(bf16[32,48,384]{2,1,0:T(8,128)(2,1)S(1)} %bitcast.159), channel_id=1, replica_groups=mesh['pipe'=4,'z'=8,'y'=4,'core'=2] {'pipe','y','core'}, dimensions={0} | all-to-all | bytes 2359296 | tf_op jit(solution)/shard_map/all_to_all | solution.py:232
  32.0 9.0 %collective-permute-done.6 = bf16[384,384]{1,0:T(8,128)(2,1)S(1)} collective-permute-done((bf16[384,384]{1,0:T(8,128)(2,1)S(1)}, bf16[384,384]{1,0:T(8,128)(2,1)S(1)}, u32[]{:S(2)}, u32[]{:S(2)}) %collective-permute-start.6) | collective-permute-done | bytes 294944 | tf_op jit(solution)/shard_map/ppermute | solution.py:193
  41.0 8.2 %collective-permute-done.7 = bf16[384,384]{1,0:T(8,128)(2,1)S(1)} collective-permute-done((bf16[384,384]{1,0:T(8,128)(2,1)S(1)}, bf16[384,384]{1,0:T(8,128)(2,1)S(1)}, u32[]{:S(2)}, u32[]{:S(2)}) %collective-permute-start.7) | collective-permute-done | bytes 294944 | tf_op jit(solution)/shard_map/ppermute | solution.py:189
  51.4 24.2 %collective-permute-done.8.refs_7_ = bf16[4,384,384]{2,1,0:T(8,128)(2,1)S(1)} collective-permute-done((bf16[4,384,384]{2,1,0:T(8,128)(2,1)S(1)}, bf16[4,384,384]{2,1,0:T(8,128)(2,1)S(1)}, u32[]{:S(2)}, u32[]{:S(2)}) %collective-permute-start.8) | collective-permute-done | bytes 1179680 | tf_op jit(solution)/shard_map/ppermute | solution.py:181
  86.8 17.2 %collective-permute-done.9.refs_8_ = bf16[4,384,384]{2,1,0:T(8,128)(2,1)} collective-permute-done((bf16[4,384,384]{2,1,0:T(8,128)(2,1)S(1)}, bf16[4,384,384]{2,1,0:T(8,128)(2,1)}, u32[]{:S(2)}, u32[]{:S(2)}) %collective-permute-start.9) | collective-permute-done | bytes 1179680 | tf_op jit(solution)/shard_map/ppermute | solution.py:181
  109.1 3.8 collective-permute-start.28
  117.6 20.7 %collective-permute-done.28 = bf16[384,384]{1,0:T(8,128)(2,1)} collective-permute-done((bf16[384,384]{1,0:T(8,128)(2,1)}, bf16[384,384]{1,0:T(8,128)(2,1)}, u32[]{:S(2)}, u32[]{:S(2)}) %collective-permute-start.28) | collective-permute-done | bytes 294944 | tf_op jit(solution)/shard_map/ppermute | solution.py:185
  148.6 4.1 collective-permute-done.26
  152.8 15.7 %collective-permute-done.30 = bf16[384,384]{1,0:T(8,128)(2,1)S(1)} collective-permute-done((bf16[384,384]{1,0:T(8,128)(2,1)S(1)}, bf16[384,384]{1,0:T(8,128)(2,1)S(1)}, u32[]{:S(2)}, u32[]{:S(2)}) %collective-permute-start.30) | collective-permute-done | bytes 294944 | tf_op jit(solution)/shard_map/ppermute | solution.py:185
  168.6 14.0 %shard_map.73 = (bf16[4,32,3072]{2,1,0:T(8,128)(2,1)S(1)}, bf16[4,32,3072]{2,1,0:T(8,128)(2,1)S(1)}) custom-call(s32[16]{0:T(128)S(1)} %stack.149.ctl, bf16[32,3072]{1,0:T(8,128)(2,1)} %fusion.4.refs_0_, bf16[32,3072]{1,0:T(8,128)(2,1)} %collective-permute-done.refs_1_, bf16[32,3072]{1,0:T(8,128)(2,1)} %collective-permute-done.1.refs_2_, ...), custom_call_target="tpu_custom_call" | custom-call | flops 2415919104 | bytes 14155776 | tf_op jit(solution)/shard_map/pallas_call | solution.py:141
  195.1 51.3 %collective-permute-done.46 = bf16[384,384]{1,0:T(8,128)(2,1)S(1)} collective-permute-done((bf16[384,384]{1,0:T(8,128)(2,1)S(1)}, bf16[384,384]{1,0:T(8,128)(2,1)S(1)}, u32[]{:S(2)}, u32[]{:S(2)}) %collective-permute-start.46) | collective-permute-done | bytes 294944 | tf_op jit(solution)/shard_map/ppermute | solution.py:193
  251.4 4.8 collective-permute-done.45
  256.2 4.3 collective-permute-done.47
  267.9 4.5 collective-permute-done.21.refs_2_
  272.6 15.3 %collective-permute-done.48.refs_7_ = bf16[4,384,384]{2,1,0:T(8,128)(2,1)S(1)} collective-permute-done((bf16[4,384,384]{2,1,0:T(8,128)(2,1)S(1)}, bf16[4,384,384]{2,1,0:T(8,128)(2,1)S(1)}, u32[]{:S(2)}, u32[]{:S(2)}) %collective-permute-start.48) | collective-permute-done | bytes 1179680 | tf_op jit(solution)/shard_map/ppermute | solution.py:181
  289.6 4.0 collective-permute-done.22.refs_3_
  296.8 12.8 %shard_map.74 = (bf16[4,32,3072]{2,1,0:T(8,128)(2,1)S(1)}, bf16[4,32,3072]{2,1,0:T(8,128)(2,1)S(1)}) custom-call(s32[16]{0:T(128)S(1)} %stack.149.ctl, bf16[32,3072]{1,0:T(8,128)(2,1)S(1)} %fusion.8.refs_0_, bf16[32,3072]{1,0:T(8,128)(2,1)S(1)} %collective-permute-done.20.refs_1_, bf16[32,3072]{1,0:T(8,128)(2,1)S(1)} %collective-permute-done.21.refs_2_, ...), custom_call_target="tpu_custom_call" | custom-call | flops 2415919104 | bytes 14155776 | tf_op jit(solution)/shard_map/pallas_call | solution.py:141
  313.1 16.4 %collective-permute-done.65 = bf16[384,384]{1,0:T(8,128)(2,1)S(1)} collective-permute-done((bf16[384,384]{1,0:T(8,128)(2,1)S(1)}, bf16[384,384]{1,0:T(8,128)(2,1)S(1)}, u32[]{:S(2)}, u32[]{:S(2)}) %collective-permute-start.65) | collective-permute-done | bytes 294944 | tf_op jit(solution)/shard_map/ppermute | solution.py:181
  332.5 6.8 %collective-permute-done.66 = bf16[384,384]{1,0:T(8,128)(2,1)S(1)} collective-permute-done((bf16[384,384]{1,0:T(8,128)(2,1)S(1)}, bf16[384,384]{1,0:T(8,128)(2,1)S(1)}, u32[]{:S(2)}, u32[]{:S(2)}) %collective-permute-start.66) | collective-permute-done | bytes 294944 | tf_op jit(solution)/shard_map/ppermute | solution.py:181
  347.6 4.3 collective-permute-done.38
  355.7 17.7 %collective-permute-done.50.refs_9_ = bf16[4,384,384]{2,1,0:T(8,128)(2,1)S(1)} collective-permute-done((bf16[4,384,384]{2,1,0:T(8,128)(2,1)S(1)}, bf16[4,384,384]{2,1,0:T(8,128)(2,1)S(1)}, u32[]{:S(2)}, u32[]{:S(2)}) %collective-permute-start.50) | collective-permute-done | bytes 1179680 | tf_op jit(solution)/shard_map/ppermute | solution.py:181
  386.2 3.3 collective-permute-start.71
  389.5 7.0 %collective-permute-done.42.refs_3_ = bf16[32,3072]{1,0:T(8,128)(2,1)S(1)} collective-permute-done((bf16[32,3072]{1,0:T(8,128)(2,1)S(1)}, bf16[32,3072]{1,0:T(8,128)(2,1)S(1)}, u32[]{:S(2)}, u32[]{:S(2)}) %collective-permute-start.42) | collective-permute-done | bytes 196640 | tf_op jit(solution)/shard_map/ppermute | solution.py:24
  397.9 13.8 %shard_map.75 = (bf16[4,32,3072]{2,1,0:T(8,128)(2,1)S(1)}, bf16[4,32,3072]{2,1,0:T(8,128)(2,1)S(1)}) custom-call(s32[16]{0:T(128)S(1)} %stack.149.ctl, bf16[32,3072]{1,0:T(8,128)(2,1)S(1)} %fusion.11.refs_0_, bf16[32,3072]{1,0:T(8,128)(2,1)S(1)} %collective-permute-done.40.refs_1_, bf16[32,3072]{1,0:T(8,128)(2,1)S(1)} %collective-permute-done.41.refs_2_, ...), custom_call_target="tpu_custom_call" | custom-call | flops 2415919104 | bytes 14155776 | tf_op jit(solution)/shard_map/pallas_call | solution.py:141
  416.5 5.7 %collective-permute-done.58 = bf16[32,3072]{1,0:T(8,128)(2,1)S(1)} collective-permute-done((bf16[32,3072]{1,0:T(8,128)(2,1)S(1)}, bf16[32,3072]{1,0:T(8,128)(2,1)S(1)}, u32[]{:S(2)}, u32[]{:S(2)}) %collective-permute-start.58) | collective-permute-done | bytes 196640 | tf_op jit(solution)/shard_map/ppermute | solution.py:24
  424.4 42.5 %collective-permute-done.73.refs_8_ = bf16[8,384,384]{2,1,0:T(8,128)(2,1)S(1)} collective-permute-done((bf16[8,384,384]{2,1,0:T(8,128)(2,1)S(1)}, bf16[8,384,384]{2,1,0:T(8,128)(2,1)S(1)}, u32[]{:S(2)}, u32[]{:S(2)}) %collective-permute-start.73) | collective-permute-done | bytes 2359328 | tf_op jit(solution)/shard_map/ppermute | solution.py:193
  471.9 3.3 collective-permute-done.60.refs_1_
  477.5 6.7 %collective-permute-done.62.refs_3_ = bf16[32,3072]{1,0:T(8,128)(2,1)S(1)} collective-permute-done((bf16[32,3072]{1,0:T(8,128)(2,1)S(1)}, bf16[32,3072]{1,0:T(8,128)(2,1)S(1)}, u32[]{:S(2)}, u32[]{:S(2)}) %collective-permute-start.62) | collective-permute-done | bytes 196640 | tf_op jit(solution)/shard_map/ppermute | solution.py:24
  484.1 10.3 %collective-permute-done.74.refs_9_ = bf16[4,384,384]{2,1,0:T(8,128)(2,1)S(1)} collective-permute-done((bf16[4,384,384]{2,1,0:T(8,128)(2,1)S(1)}, bf16[4,384,384]{2,1,0:T(8,128)(2,1)S(1)}, u32[]{:S(2)}, u32[]{:S(2)}) %collective-permute-start.74) | collective-permute-done | bytes 1179680 | tf_op jit(solution)/shard_map/ppermute | solution.py:189
  495.9 12.8 %shard_map.76 = (bf16[4,32,3072]{2,1,0:T(8,128)(2,1)S(1)}, bf16[4,32,3072]{2,1,0:T(8,128)(2,1)S(1)}) custom-call(s32[16]{0:T(128)S(1)} %stack.149.ctl, bf16[32,3072]{1,0:T(8,128)(2,1)S(1)} %fusion.14.refs_0_, bf16[32,3072]{1,0:T(8,128)(2,1)S(1)} %collective-permute-done.60.refs_1_, bf16[32,3072]{1,0:T(8,128)(2,1)S(1)} %collective-permute-done.61.refs_2_, ...), custom_call_target="tpu_custom_call" | custom-call | flops 2415919104 | bytes 14155776 | tf_op jit(solution)/shard_map/pallas_call | solution.py:141
  513.4 5.7 %collective-permute-done.78 = bf16[32,3072]{1,0:T(8,128)(2,1)S(1)} collective-permute-done((bf16[32,3072]{1,0:T(8,128)(2,1)S(1)}, bf16[32,3072]{1,0:T(8,128)(2,1)S(1)}, u32[]{:S(2)}, u32[]{:S(2)}) %collective-permute-start.78) | collective-permute-done | bytes 196640 | tf_op jit(solution)/shard_map/ppermute | solution.py:24
  522.6 3.6 collective-permute-done.79
  (216 shorter events, 128.0 us)
Async XLA Ops:
  49.3 26.4 %collective-permute-start.8 = (bf16[4,384,384]{2,1,0:T(8,128)(2,1)S(1)}, bf16[4,384,384]{2,1,0:T(8,128)(2,1)S(1)}, u32[]{:S(2)}, u32[]{:S(2)}) collective-permute-start(bf16[4,384,384]{2,1,0:T(8,128)(2,1)S(1)} %pad_maximum_fusion.refs_6_), channel_id=1, source_target_pairs={{0,8},{8,16},{16,24},{24,32},{32,40},{40,48},{48,56},{56,0},{1,9},... | collective-permute-start | bytes 3538952 | tf_op jit(solution)/shard_map/ppermute | solution.py:181
  51.3 27.3 %collective-permute-start.11 = (bf16[4,384,384]{2,1,0:T(8,128)(2,1)S(1)}, bf16[4,384,384]{2,1,0:T(8,128)(2,1)S(1)}, u32[]{:S(2)}, u32[]{:S(2)}) collective-permute-start(bf16[4,384,384]{2,1,0:T(8,128)(2,1)S(1)} %pad_maximum_fusion.refs_6_), channel_id=1, source_target_pairs={{0,56},{8,0},{16,8},{24,16},{32,24},{40,32},{48,40},{56,48},{1,57}... | collective-permute-start | bytes 3538952 | tf_op jit(solution)/shard_map/ppermute | solution.py:185
  75.7 28.3 %collective-permute-start.9 = (bf16[4,384,384]{2,1,0:T(8,128)(2,1)S(1)}, bf16[4,384,384]{2,1,0:T(8,128)(2,1)}, u32[]{:S(2)}, u32[]{:S(2)}) collective-permute-start(bf16[4,384,384]{2,1,0:T(8,128)(2,1)S(1)} %collective-permute-done.8.refs_7_), channel_id=1, source_target_pairs={{0,8},{8,16},{16,24},{24,32},{32,40},{40,48},{48,56},{56,0},{1,9},... | collective-permute-start | bytes 3538952 | tf_op jit(solution)/shard_map/ppermute | solution.py:181
  78.6 26.1 %collective-permute-start.12 = (bf16[4,384,384]{2,1,0:T(8,128)(2,1)S(1)}, bf16[4,384,384]{2,1,0:T(8,128)(2,1)}, u32[]{:S(2)}, u32[]{:S(2)}) collective-permute-start(bf16[4,384,384]{2,1,0:T(8,128)(2,1)S(1)} %collective-permute-done.11.refs_10_), channel_id=1, source_target_pairs={{0,56},{8,0},{16,8},{24,16},{32,24},{40,32},{48,40},{56,48},{1,57}... | collective-permute-start | bytes 3538952 | tf_op jit(solution)/shard_map/ppermute | solution.py:185
  104.0 37.1 %collective-permute-start.10 = (bf16[4,384,384]{2,1,0:T(8,128)(2,1)}, bf16[4,384,384]{2,1,0:T(8,128)(2,1)S(1)}, u32[]{:S(2)}, u32[]{:S(2)}) collective-permute-start(bf16[4,384,384]{2,1,0:T(8,128)(2,1)} %collective-permute-done.9.refs_8_), channel_id=1, source_target_pairs={{0,8},{8,16},{16,24},{24,32},{32,40},{40,48},{48,56},{56,0},{1,9},... | collective-permute-start | bytes 3538952 | tf_op jit(solution)/shard_map/ppermute | solution.py:181
  104.7 37.7 %collective-permute-start.13 = (bf16[4,384,384]{2,1,0:T(8,128)(2,1)}, bf16[4,384,384]{2,1,0:T(8,128)(2,1)S(1)}, u32[]{:S(2)}, u32[]{:S(2)}) collective-permute-start(bf16[4,384,384]{2,1,0:T(8,128)(2,1)} %collective-permute-done.12.refs_11_), channel_id=1, source_target_pairs={{0,56},{8,0},{16,8},{24,16},{32,24},{40,32},{48,40},{56,48},{1,57}... | collective-permute-start | bytes 3538952 | tf_op jit(solution)/shard_map/ppermute | solution.py:185
  109.1 29.1 %collective-permute-start.28 = (bf16[384,384]{1,0:T(8,128)(2,1)}, bf16[384,384]{1,0:T(8,128)(2,1)}, u32[]{:S(2)}, u32[]{:S(2)}) collective-permute-start(bf16[384,384]{1,0:T(8,128)(2,1)} %bitcast.169), channel_id=1, source_target_pairs={{0,56},{8,0},{16,8},{24,16},{32,24},{40,32},{48,40},{56,48},{1,57}... | collective-permute-start | bytes 884744 | tf_op jit(solution)/shard_map/ppermute | solution.py:185
  117.2 28.3 %collective-permute-start.4 = (bf16[32,3072]{1,0:T(8,128)(2,1)}, bf16[32,3072]{1,0:T(8,128)(2,1)S(1)}, u32[]{:S(2)}, u32[]{:S(2)}) collective-permute-start(bf16[32,3072]{1,0:T(8,128)(2,1)} %collective-permute-done.2.refs_3_), channel_id=1, source_target_pairs={{0,1},{1,0},{2,3},{3,2},{4,5},{5,4},{6,7},{7,6},{8,9},{9,8},{10,11... | collective-permute-start | bytes 589832 | tf_op jit(solution)/shard_map/ppermute | solution.py:32
  141.0 27.5 %collective-permute-start.3 = (bf16[3,32,3072]{2,1,0:T(8,128)(2,1)S(1)}, bf16[3,32,3072]{2,1,0:T(8,128)(2,1)S(1)}, u32[]{:S(2)}, u32[]{:S(2)}) collective-permute-start(bf16[3,32,3072]{2,1,0:T(8,128)(2,1)S(1)} %pad_maximum_fusion.2), channel_id=1, source_target_pairs={{0,1},{1,0},{2,3},{3,2},{4,5},{5,4},{6,7},{7,6},{8,9},{9,8},{10,11... | collective-permute-start | bytes 1769480 | tf_op jit(solution)/shard_map/ppermute | solution.py:32
  142.4 26.1 %collective-permute-start.14 = (bf16[2,384,384]{2,1,0:T(8,128)(2,1)S(1)}, bf16[2,384,384]{2,1,0:T(8,128)(2,1)S(1)}, u32[]{:S(2)}, u32[]{:S(2)}) collective-permute-start(bf16[2,384,384]{2,1,0:T(8,128)(2,1)S(1)} %slice.129), channel_id=1, source_target_pairs={{0,8},{8,16},{16,24},{24,32},{32,40},{40,48},{48,56},{56,0},{1,9},... | collective-permute-start | bytes 1769480 | tf_op jit(solution)/shard_map/ppermute | solution.py:181
  152.7 30.0 %collective-permute-start.27 = (bf16[384,384]{1,0:T(8,128)(2,1)S(1)}, bf16[384,384]{1,0:T(8,128)(2,1)S(1)}, u32[]{:S(2)}, u32[]{:S(2)}) collective-permute-start(bf16[384,384]{1,0:T(8,128)(2,1)S(1)} %collective-permute-done.26), channel_id=1, source_target_pairs={{0,8},{8,16},{16,24},{24,32},{32,40},{40,48},{48,56},{56,0},{1,9},... | collective-permute-start | bytes 884744 | tf_op jit(solution)/shard_map/ppermute | solution.py:181
  185.7 78.0 %collective-permute-start.33 = (bf16[8,384,384]{2,1,0:T(8,128)(2,1)S(1)}, bf16[8,384,384]{2,1,0:T(8,128)(2,1)S(1)}, u32[]{:S(2)}, u32[]{:S(2)}) collective-permute-start(bf16[8,384,384]{2,1,0:T(8,128)(2,1)S(1)} %bitcast_dynamic-update-slice_fusion.8.refs_6_), channel_id=1, source_target_pairs={{64,128},{128,64},{192,0},{0,192},{65,129},{129,65},{193,1},{1,193... | collective-permute-start | bytes 7077896 | tf_op jit(solution)/shard_map/ppermute | solution.py:193
  186.9 77.3 %collective-permute-start.32 = (bf16[8,384,384]{2,1,0:T(8,128)(2,1)S(1)}, bf16[8,384,384]{2,1,0:T(8,128)(2,1)S(1)}, u32[]{:S(2)}, u32[]{:S(2)}) collective-permute-start(bf16[8,384,384]{2,1,0:T(8,128)(2,1)S(1)} %bitcast_dynamic-update-slice_fusion.8.refs_6_), channel_id=1, source_target_pairs={{0,64},{64,0},{128,192},{192,128},{1,65},{65,1},{129,193},{193,129... | collective-permute-start | bytes 7077896 | tf_op jit(solution)/shard_map/ppermute | solution.py:189
  187.2 59.2 %collective-permute-start.46 = (bf16[384,384]{1,0:T(8,128)(2,1)S(1)}, bf16[384,384]{1,0:T(8,128)(2,1)S(1)}, u32[]{:S(2)}, u32[]{:S(2)}) collective-permute-start(bf16[384,384]{1,0:T(8,128)(2,1)S(1)} %bitcast.160), channel_id=1, source_target_pairs={{64,128},{128,64},{192,0},{0,192},{65,129},{129,65},{193,1},{1,193... | collective-permute-start | bytes 884744 | tf_op jit(solution)/shard_map/ppermute | solution.py:193
  189.7 56.6 %collective-permute-start.17 = (bf16[32,3072]{1,0:T(8,128)(2,1)S(1)}, bf16[32,3072]{1,0:T(8,128)(2,1)S(1)}, u32[]{:S(2)}, u32[]{:S(2)}) collective-permute-start(bf16[32,3072]{1,0:T(8,128)(2,1)S(1)} %get-tuple-element.37), channel_id=1, source_target_pairs={{0,2},{2,0},{4,6},{6,4},{1,3},{3,1},{5,7},{7,5},{8,10},{10,8},{12,... | collective-permute-start | bytes 589832 | tf_op jit(solution)/shard_map/ppermute | solution.py:24
  193.1 55.3 %collective-permute-start.19 = (bf16[32,3072]{1,0:T(8,128)(2,1)S(1)}, bf16[32,3072]{1,0:T(8,128)(2,1)S(1)}, u32[]{:S(2)}, u32[]{:S(2)}) collective-permute-start(bf16[32,3072]{1,0:T(8,128)(2,1)S(1)} %fusion.22), channel_id=1, source_target_pairs={{2,4},{4,2},{6,0},{0,6},{3,5},{5,3},{7,1},{1,7},{10,12},{12,10},{1... | collective-permute-start | bytes 589832 | tf_op jit(solution)/shard_map/ppermute | solution.py:28
  260.8 27.2 %collective-permute-start.48 = (bf16[4,384,384]{2,1,0:T(8,128)(2,1)S(1)}, bf16[4,384,384]{2,1,0:T(8,128)(2,1)S(1)}, u32[]{:S(2)}, u32[]{:S(2)}) collective-permute-start(bf16[4,384,384]{2,1,0:T(8,128)(2,1)S(1)} %pad_maximum_fusion.1.refs_6_), channel_id=1, source_target_pairs={{0,8},{8,16},{16,24},{24,32},{32,40},{40,48},{48,56},{56,0},{1,9},... | collective-permute-start | bytes 3538952 | tf_op jit(solution)/shard_map/ppermute | solution.py:181
  262.8 30.8 %collective-permute-start.51 = (bf16[4,384,384]{2,1,0:T(8,128)(2,1)S(1)}, bf16[4,384,384]{2,1,0:T(8,128)(2,1)S(1)}, u32[]{:S(2)}, u32[]{:S(2)}) collective-permute-start(bf16[4,384,384]{2,1,0:T(8,128)(2,1)S(1)} %pad_maximum_fusion.1.refs_6_), channel_id=1, source_target_pairs={{0,56},{8,0},{16,8},{24,16},{32,24},{40,32},{48,40},{56,48},{1,57}... | collective-permute-start | bytes 3538952 | tf_op jit(solution)/shard_map/ppermute | solution.py:185
  263.9 30.7 %collective-permute-start.34 = (bf16[4,384,384]{2,1,0:T(8,128)(2,1)S(1)}, bf16[4,384,384]{2,1,0:T(8,128)(2,1)S(1)}, u32[]{:S(2)}, u32[]{:S(2)}) collective-permute-start(bf16[4,384,384]{2,1,0:T(8,128)(2,1)S(1)} %slice.136), channel_id=1, source_target_pairs={{0,64},{64,0},{128,192},{192,128},{1,65},{65,1},{129,193},{193,129... | collective-permute-start | bytes 3538952 | tf_op jit(solution)/shard_map/ppermute | solution.py:189
  264.4 32.5 %collective-permute-start.35 = (bf16[4,384,384]{2,1,0:T(8,128)(2,1)S(1)}, bf16[4,384,384]{2,1,0:T(8,128)(2,1)S(1)}, u32[]{:S(2)}, u32[]{:S(2)}) collective-permute-start(bf16[4,384,384]{2,1,0:T(8,128)(2,1)S(1)} %slice.137), channel_id=1, source_target_pairs={{64,128},{128,64},{192,0},{0,192},{65,129},{129,65},{193,1},{1,193... | collective-permute-start | bytes 3538952 | tf_op jit(solution)/shard_map/ppermute | solution.py:193
  293.6 48.6 %collective-permute-start.49 = (bf16[4,384,384]{2,1,0:T(8,128)(2,1)S(1)}, bf16[4,384,384]{2,1,0:T(8,128)(2,1)S(1)}, u32[]{:S(2)}, u32[]{:S(2)}) collective-permute-start(bf16[4,384,384]{2,1,0:T(8,128)(2,1)S(1)} %collective-permute-done.48.refs_7_), channel_id=1, source_target_pairs={{0,8},{8,16},{16,24},{24,32},{32,40},{40,48},{48,56},{56,0},{1,9},... | collective-permute-start | bytes 3538952 | tf_op jit(solution)/shard_map/ppermute | solution.py:181
  294.5 48.1 %collective-permute-start.52 = (bf16[4,384,384]{2,1,0:T(8,128)(2,1)S(1)}, bf16[4,384,384]{2,1,0:T(8,128)(2,1)S(1)}, u32[]{:S(2)}, u32[]{:S(2)}) collective-permute-start(bf16[4,384,384]{2,1,0:T(8,128)(2,1)S(1)} %collective-permute-done.51.refs_10_), channel_id=1, source_target_pairs={{0,56},{8,0},{16,8},{24,16},{32,24},{40,32},{48,40},{56,48},{1,57}... | collective-permute-start | bytes 3538952 | tf_op jit(solution)/shard_map/ppermute | solution.py:185
  309.7 35.9 %collective-permute-start.36 = (bf16[4,32,3072]{2,1,0:T(8,128)(2,1)S(1)}, bf16[4,32,3072]{2,1,0:T(8,128)(2,1)S(1)}, u32[]{:S(2)}, u32[]{:S(2)}) collective-permute-start(bf16[4,32,3072]{2,1,0:T(8,128)(2,1)S(1)} %get-tuple-element.16), channel_id=1, source_target_pairs={{0,1},{1,0},{2,3},{3,2},{4,5},{5,4},{6,7},{7,6},{8,9},{9,8},{10,11... | collective-permute-start | bytes 2359304 | tf_op jit(solution)/shard_map/ppermute | solution.py:32
  339.9 46.3 %collective-permute-start.70 = (bf16[384,384]{1,0:T(8,128)(2,1)S(1)}, bf16[384,384]{1,0:T(8,128)(2,1)S(1)}, u32[]{:S(2)}, u32[]{:S(2)}) collective-permute-start(bf16[384,384]{1,0:T(8,128)(2,1)S(1)} %collective-permute-done.69), channel_id=1, source_target_pairs={{0,56},{8,0},{16,8},{24,16},{32,24},{40,32},{48,40},{56,48},{1,57}... | collective-permute-start | bytes 884744 | tf_op jit(solution)/shard_map/ppermute | solution.py:185
  342.2 31.2 %collective-permute-start.50 = (bf16[4,384,384]{2,1,0:T(8,128)(2,1)S(1)}, bf16[4,384,384]{2,1,0:T(8,128)(2,1)S(1)}, u32[]{:S(2)}, u32[]{:S(2)}) collective-permute-start(bf16[4,384,384]{2,1,0:T(8,128)(2,1)S(1)} %collective-permute-done.49.refs_8_), channel_id=1, source_target_pairs={{0,8},{8,16},{16,24},{24,32},{32,40},{40,48},{48,56},{56,0},{1,9},... | collective-permute-start | bytes 3538952 | tf_op jit(solution)/shard_map/ppermute | solution.py:181
  342.7 31.2 %collective-permute-start.53 = (bf16[4,384,384]{2,1,0:T(8,128)(2,1)S(1)}, bf16[4,384,384]{2,1,0:T(8,128)(2,1)S(1)}, u32[]{:S(2)}, u32[]{:S(2)}) collective-permute-start(bf16[4,384,384]{2,1,0:T(8,128)(2,1)S(1)} %collective-permute-done.52.refs_11_), channel_id=1, source_target_pairs={{0,56},{8,0},{16,8},{24,16},{32,24},{40,32},{48,40},{56,48},{1,57}... | collective-permute-start | bytes 3538952 | tf_op jit(solution)/shard_map/ppermute | solution.py:185
  412.0 54.8 %collective-permute-start.73 = (bf16[8,384,384]{2,1,0:T(8,128)(2,1)S(1)}, bf16[8,384,384]{2,1,0:T(8,128)(2,1)S(1)}, u32[]{:S(2)}, u32[]{:S(2)}) collective-permute-start(bf16[8,384,384]{2,1,0:T(8,128)(2,1)S(1)} %bitcast_dynamic-update-slice_fusion.refs_6_), channel_id=1, source_target_pairs={{64,128},{128,64},{192,0},{0,192},{65,129},{129,65},{193,1},{1,193... | collective-permute-start | bytes 7077896 | tf_op jit(solution)/shard_map/ppermute | solution.py:193
  413.3 53.8 %collective-permute-start.72 = (bf16[8,384,384]{2,1,0:T(8,128)(2,1)S(1)}, bf16[8,384,384]{2,1,0:T(8,128)(2,1)S(1)}, u32[]{:S(2)}, u32[]{:S(2)}) collective-permute-start(bf16[8,384,384]{2,1,0:T(8,128)(2,1)S(1)} %bitcast_dynamic-update-slice_fusion.refs_6_), channel_id=1, source_target_pairs={{0,64},{64,0},{128,192},{192,128},{1,65},{65,1},{129,193},{193,129... | collective-permute-start | bytes 7077896 | tf_op jit(solution)/shard_map/ppermute | solution.py:189
  414.7 54.1 %collective-permute-start.57 = (bf16[32,3072]{1,0:T(8,128)(2,1)S(1)}, bf16[32,3072]{1,0:T(8,128)(2,1)S(1)}, u32[]{:S(2)}, u32[]{:S(2)}) collective-permute-start(bf16[32,3072]{1,0:T(8,128)(2,1)S(1)} %get-tuple-element.33), channel_id=1, source_target_pairs={{0,2},{2,0},{4,6},{6,4},{1,3},{3,1},{5,7},{7,5},{8,10},{10,8},{12,... | collective-permute-start | bytes 589832 | tf_op jit(solution)/shard_map/ppermute | solution.py:24
  422.3 46.5 %collective-permute-start.59 = (bf16[32,3072]{1,0:T(8,128)(2,1)S(1)}, bf16[32,3072]{1,0:T(8,128)(2,1)S(1)}, u32[]{:S(2)}, u32[]{:S(2)}) collective-permute-start(bf16[32,3072]{1,0:T(8,128)(2,1)S(1)} %fusion.18), channel_id=1, source_target_pairs={{2,4},{4,2},{6,0},{0,6},{3,5},{5,3},{7,1},{1,7},{10,12},{12,10},{1... | collective-permute-start | bytes 589832 | tf_op jit(solution)/shard_map/ppermute | solution.py:28
  467.0 27.5 %collective-permute-start.74 = (bf16[4,384,384]{2,1,0:T(8,128)(2,1)S(1)}, bf16[4,384,384]{2,1,0:T(8,128)(2,1)S(1)}, u32[]{:S(2)}, u32[]{:S(2)}) collective-permute-start(bf16[4,384,384]{2,1,0:T(8,128)(2,1)S(1)} %slice.150), channel_id=1, source_target_pairs={{0,64},{64,0},{128,192},{192,128},{1,65},{65,1},{129,193},{193,129... | collective-permute-start | bytes 3538952 | tf_op jit(solution)/shard_map/ppermute | solution.py:189
  467.2 28.7 %collective-permute-start.75 = (bf16[4,384,384]{2,1,0:T(8,128)(2,1)S(1)}, bf16[4,384,384]{2,1,0:T(8,128)(2,1)S(1)}, u32[]{:S(2)}, u32[]{:S(2)}) collective-permute-start(bf16[4,384,384]{2,1,0:T(8,128)(2,1)S(1)} %slice.151), channel_id=1, source_target_pairs={{64,128},{128,64},{192,0},{0,192},{65,129},{129,65},{193,1},{1,193... | collective-permute-start | bytes 3538952 | tf_op jit(solution)/shard_map/ppermute | solution.py:193
  (55 other events, 705.5 us)
